TPU v7x, 768 devices: a whole 4x8x12 slice. The times are simulated.
768 devices in a mesh: gx: 64 (over y, x, core), gz: 12 (over z).
Axes of the slice: x: 4, y: 8, z: 12, core: 2. Of those that a mesh axis runs over, the one named last changes fastest.
Arguments:
- velocity: bfloat16 [2, 128, 2, 1536, 1536], P(None, None, None, 'gx', 'gz'), may hold values from -8 to 8
- snapshot_rank: int32 [128], replicated, may hold values from 0 to 127, each once
- anchor_index: int32 [64], replicated, may hold values from 0 to 4718591
- start_basis: float32 [128, 64], replicated, may hold values from -6 to 6
Outputs:
- modes: bfloat16 [64, 2, 1536, 1536], P(None, None, 'gx', 'gz')
- basis: float32 [128, 64], replicated
All inputs are finite; a program needn't handle non-finite values.
Results may differ from a plain program's by a relative error of at most 0.0073.
Values may be sent and summed in bfloat16 or wider, within the bound.
No kernel may reach another device: no remote copies, remote signals or barrier semaphores. Data moves between devices by JAX's collectives and lax.ppermute only.
A program may use at most 32 MiB of HBM per device.

v0:
```python
import jax
import jax.numpy as jnp
from jax import lax
from jax.sharding import PartitionSpec as P

ITERS = 3


def extended(cells, sides, width):
    for axis, dim in sides:
        count = lax.axis_size(axis)
        head = lax.slice_in_dim(cells, 0, width, axis=dim)
        tail = lax.slice_in_dim(cells, cells.shape[dim] - width, cells.shape[dim], axis=dim)
        cells = jnp.concatenate(
            [
                lax.ppermute(tail, axis, [(i, (i + 1) % count) for i in range(count)]),
                cells,
                lax.ppermute(head, axis, [((i + 1) % count, i) for i in range(count)]),
            ],
            axis=dim,
        )
    return cells


def orthonormal(block):
    inner = jnp.dot(block.T, block, precision=lax.Precision.HIGHEST)
    lower = jnp.linalg.cholesky(inner)
    return jax.scipy.linalg.solve_triangular(lower, block.T, lower=True).T


def body(velocity, snapshot_rank, anchor_index, start_basis):
    snaps = velocity.shape[1]
    planes = velocity.shape[2]
    cols_x = velocity.shape[3]
    cols_z = velocity.shape[4]
    kept = start_basis.shape[1]
    wide_w = extended(velocity[1], (("gx", 2),), 3)
    wide_u = extended(velocity[0], (("gz", 3),), 3)
    weights = (45.0 / 60.0, -9.0 / 60.0, 1.0 / 60.0)
    total = jnp.zeros((snaps, planes, cols_x, cols_z), jnp.float32)
    for shift_by in range(1, 4):
        weight_now = weights[shift_by - 1]
        ahead_w = wide_w[:, :, 3 + shift_by : 3 + shift_by + cols_x, :].astype(jnp.float32)
        behind_w = wide_w[:, :, 3 - shift_by : 3 - shift_by + cols_x, :].astype(jnp.float32)
        ahead_u = wide_u[:, :, :, 3 + shift_by : 3 + shift_by + cols_z].astype(jnp.float32)
        behind_u = wide_u[:, :, :, 3 - shift_by : 3 - shift_by + cols_z].astype(jnp.float32)
        total = total + weight_now * (ahead_w - behind_w) - weight_now * (ahead_u - behind_u)
    flat = total.astype(jnp.bfloat16).reshape(snaps, planes * cols_x * cols_z)
    local_gram = lax.dot_general(
        flat, flat, (((1,), (1,)), ((), ())), preferred_element_type=jnp.float32
    )
    gram = lax.psum(local_gram, ("gx", "gz"))
    count_x = lax.axis_size("gx")
    count_z = lax.axis_size("gz")
    total_x = cols_x * count_x
    total_z = cols_z * count_z
    gram = gram / float(planes * total_x * total_z)
    scale = jnp.where(snapshot_rank < kept, 1.0, 0.25).astype(jnp.float32)
    weighted = scale[:, None] * gram * scale[None, :]
    basis_now = start_basis
    for step in range(ITERS):
        basis_now = orthonormal(jnp.dot(weighted, basis_now, precision=lax.Precision.HIGHEST))
    coef = (scale[:, None] * basis_now).astype(jnp.bfloat16)
    raw = lax.dot_general(coef, flat, (((0,), (0,)), ((), ())), preferred_element_type=jnp.float32)
    plane_of = anchor_index // (total_x * total_z)
    remain = anchor_index % (total_x * total_z)
    local_x = remain // total_z - lax.axis_index("gx") * cols_x
    local_z = remain % total_z - lax.axis_index("gz") * cols_z
    owned = (local_x >= 0) & (local_x < cols_x) & (local_z >= 0) & (local_z < cols_z)
    position = (plane_of * cols_x + jnp.clip(local_x, 0, cols_x - 1)) * cols_z + jnp.clip(
        local_z, 0, cols_z - 1
    )
    values = jnp.take_along_axis(raw, position[:, None], axis=1)[:, 0]
    term = jnp.where(owned, values, 0.0)
    anchor = lax.psum(term, ("gx", "gz"))
    orient = anchor / jnp.maximum(jnp.abs(anchor), 1.0)
    modes = (raw * orient[:, None]).astype(jnp.bfloat16).reshape(kept, planes, cols_x, cols_z)
    return (modes, basis_now * orient[None, :])


def solution(mesh):
    return jax.shard_map(
        body,
        mesh=mesh,
        in_specs=(P(None, None, None, "gx", "gz"), P(), P(), P()),
        out_specs=(P(None, None, "gx", "gz"), P()),
        check_vma=False,
    )
```

profile of v0, /device:TPU:1, one launch (start us, length us, event | category | flops | bytes accessed | tf_op | source)
XLA Modules:
  0.0 660.1 jit_solution(7704084092897013314)
XLA Ops:
  7.2 3.6 fusion.43
  10.8 1.1 copy.37
  11.9 0.8 fusion.44
  12.7 12.4 %collective-permute-start = (bf16[128,2,3,128]{0,3,2,1:T(8,128)(2,1)}, bf16[128,2,3,128]{0,3,2,1:T(8,128)(2,1)S(1)}, u32[]{:S(2)}, u32[]{:S(2)}) collective-permute-start(bf16[128,2,3,128]{0,3,2,1:T(8,128)(2,1)} %get-tuple-element.9), channel_id=1, source_target_pairs={{12,0},{24,12},{36,24},{48,36},{60,48},{72,60},{84,72},{96,84},{10... | collective-permute-start | bytes 589832 | tf_op jit(solution)/shard_map/ppermute | solution.py:18
  25.1 1.9 collective-permute-start.1
  27.1 2.1 copy.38
  29.3 6.4 collective-permute-start.2
  35.7 1.9 collective-permute-start.3
  37.7 3.8 collective-permute-done.3
  41.6 12.7 %subtract_convert_fusion = bf16[128,2,24,128]{0,3,2,1:T(8,128)(2,1)S(1)} fusion(bf16[128,2,24,128]{0,3,2,1:T(8,128)(2,1)S(1)} %bitcast.68, bf16[128,2,24,3]{0,3,2,1:T(4,128)(2,1)S(1)} %copy.28, bf16[128,2,24,3]{0,3,2,1:T(4,128)(2,1)S(1)} %copy.26, bf16[128,2,3,128]{0,3,2,1:T(8,128)(2,1)} %collective-permute-done.1, ...), kind=kLoop, calls=%fused_computation.1 | loop fusion | flops 51904512 | bytes 5185536 | tf_op jit(solution)/shard_map/convert_element_type | solution.py:48
  54.3 1.2 convolution_bitcast_fusion
  55.6 445.0 %all-reduce.2.cloned.1.call-done = f32[128,128]{1,0:T(8,128)} async-done(((f32[128,128]{1,0:T(8,128)}), f32[128,128]{1,0:T(8,128)}) %all-reduce.2.cloned.1.call-update) | async-done | bytes 65552 | tf_op jit(solution)/shard_map/psum | solution.py:52
  500.6 1.1 fusion.11
  502.1 5.8 cholesky.59
  509.3 4.9 custom-call.9
  514.4 1.2 fusion.10
  515.9 5.8 cholesky.70
  523.1 4.9 custom-call.10
  528.2 1.2 fusion.9
  529.7 5.8 cholesky.81
  536.8 4.9 custom-call.11
  542.7 0.9 gather_fusion
  543.6 107.8 %psum.15 = f32[64]{0:T(128)S(1)} all-reduce(f32[64]{0:T(128)S(1)} %and_select_fusion.2), channel_id=1, replica_groups=mesh['gx'=64,'gz'=12] {'gx','gz'}, use_global_device_ids=true, to_apply=%region_3.6 | all-reduce | flops 64 | bytes 512 | tf_op jit(solution)/shard_map/psum | solution.py:75
  652.3 1.0 copy.39
  (49 shorter events, 7.4 us)
Async XLA Ops:
  7.2 493.5 %copy-start = (f32[128,64]{0,1:T(8,128)S(1)}, f32[128,64]{0,1:T(8,128)}, u32[]{:S(2)}) copy-start(f32[128,64]{0,1:T(8,128)} %param.10) | copy-start | bytes 98308
  7.2 493.5 %all-reduce.2.cloned.1.call-start = ((), (), s32[]{:S(2)}) async-start(), calls=%async_computation | async-start | bytes 131072 | tf_op jit(solution)/shard_map/psum | solution.py:52
  10.8 26.8 %copy-start.2 = (s32[64]{0:T(128)S(1)}, s32[64]{0:T(128)}, u32[]{:S(2)}) copy-start(s32[64]{0:T(128)} %param.9) | copy-start | bytes 772
  10.8 26.9 %copy-start.3 = (s32[128]{0:T(128)S(1)}, s32[128]{0:T(128)}, u32[]{:S(2)}) copy-start(s32[128]{0:T(128)} %param.8) | copy-start | bytes 1540
  12.7 28.9 %collective-permute-start = (bf16[128,2,3,128]{0,3,2,1:T(8,128)(2,1)}, bf16[128,2,3,128]{0,3,2,1:T(8,128)(2,1)S(1)}, u32[]{:S(2)}, u32[]{:S(2)}) collective-permute-start(bf16[128,2,3,128]{0,3,2,1:T(8,128)(2,1)} %get-tuple-element.9), channel_id=1, source_target_pairs={{12,0},{24,12},{36,24},{48,36},{60,48},{72,60},{84,72},{96,84},{10... | collective-permute-start | bytes 589832 | tf_op jit(solution)/shard_map/ppermute | solution.py:18
  25.1 16.5 %collective-permute-start.1 = (bf16[128,2,3,128]{0,3,2,1:T(8,128)(2,1)}, bf16[128,2,3,128]{0,3,2,1:T(8,128)(2,1)}, u32[]{:S(2)}, u32[]{:S(2)}) collective-permute-start(bf16[128,2,3,128]{0,3,2,1:T(8,128)(2,1)} %get-tuple-element.10), channel_id=1, source_target_pairs={{0,12},{12,24},{24,36},{36,48},{48,60},{60,72},{72,84},{84,96},{96... | collective-permute-start | bytes 589832 | tf_op jit(solution)/shard_map/ppermute | solution.py:16
  29.2 12.4 %copy-start.1 = (bf16[1,128,2,24,128]{1,4,3,2,0:T(8,128)(2,1)}, bf16[1,128,2,24,128]{1,4,3,2,0:T(8,128)(2,1)S(1)}, u32[]{:S(2)}) copy-start(bf16[1,128,2,24,128]{1,4,3,2,0:T(8,128)(2,1)S(1)} %copy.38) | copy-start | bytes 4718596
  29.3 8.4 %collective-permute-start.2 = (bf16[128,2,24,3]{0,2,3,1:T(8,128)(2,1)S(1)}, bf16[128,2,24,3]{0,2,3,1:T(8,128)(2,1)S(1)}, u32[]{:S(2)}, u32[]{:S(2)}) collective-permute-start(bf16[128,2,24,3]{0,2,3,1:T(8,128)(2,1)S(1)} %copy.25), channel_id=1, source_target_pairs={{1,0},{2,1},{3,2},{4,3},{5,4},{6,5},{7,6},{8,7},{9,8},{10,9},{11,1... | collective-permute-start | bytes 110600 | tf_op jit(solution)/shard_map/ppermute | solution.py:18
  35.7 5.9 collective-permute-start.3
Sparse Core Ops, SparseCore 0:
  55.7 444.8 all-reduce.1
where the time goes:
time: 661 us; the launch traced here: 660 us
  waiting for transfers between devices  449 us (68%)
  blocking collectives  108 us (16%)
  other arithmetic  49.9 us (8%)
  starting transfers between devices  22.7 us (3%)
  between operations  14.4 us (2%)
  local copies, waits for them, and re-layouts  9.84 us (1%)
  matrix products  6.66 us (1%)
    psum x1, waiting for transfers between devices, body(): gram = lax.psum(local_gram, ('gx', 'gz'))  445 us
    psum x1, blocking collectives, body(): anchor = lax.psum(term, ('gx', 'gz'))  108 us
    another operation x9, other arithmetic, orthonormal(): lower = jnp.linalg.cholesky(inner)  19.6 us
    ppermute x2, starting transfers between devices, extended(): lax.ppermute(head, axis, [((i + 1) % count, i) for i in range(count)])  18.8 us
    another operation x6, other arithmetic, orthonormal(): return jax.scipy.linalg.solve_triangular(lower, block.T, lower=True).T  16.6 us
  transfers between devices with their start and end apart: 5, of which 2 were waited for; matrix products, arithmetic and copies ran while one was open for 0% of the time, Pallas kernels for 0%

commit v1 on v0

--- a/solution.py
+++ b/solution.py
@@ -28,6 +28,32 @@
     return jax.scipy.linalg.solve_triangular(lower, block.T, lower=True).T
 
 
+def local_position(anchor_index, planes, cols_x, cols_z, total_x, total_z):
+    plane_of = anchor_index // (total_x * total_z)
+    remain = anchor_index % (total_x * total_z)
+    local_x = remain // total_z - lax.axis_index("gx") * cols_x
+    local_z = remain % total_z - lax.axis_index("gz") * cols_z
+    owned = (local_x >= 0) & (local_x < cols_x) & (local_z >= 0) & (local_z < cols_z)
+    return jnp.where(owned, (plane_of * cols_x + local_x) * cols_z + local_z, -1)
+
+
+def exchanged(rows, axis):
+    return lax.all_to_all(rows, axis, 0, 0, tiled=True)
+
+
+def total_of(local, snaps, kept):
+    count_x = lax.axis_size("gx")
+    count_z = lax.axis_size("gz")
+    width = local.shape[1]
+    blocks = local.shape[0] // count_x
+    rows = jnp.concatenate([local[b * count_x : (b + 1) * count_x] for b in range(blocks)], axis=1)
+    mine = jnp.sum(exchanged(rows, "gx"), axis=0)
+    mine = jnp.sum(exchanged(jnp.broadcast_to(mine, (count_z,) + mine.shape), "gz"), axis=0)
+    rows = exchanged(jnp.broadcast_to(mine, (count_x,) + mine.shape), "gx")
+    whole = jnp.concatenate([rows[:, b * width : (b + 1) * width] for b in range(blocks)], axis=0)
+    return whole[:snaps], whole[snaps:]
+
+
 def body(velocity, snapshot_rank, anchor_index, start_basis):
     snaps = velocity.shape[1]
     planes = velocity.shape[2]
@@ -46,14 +72,20 @@
         behind_u = wide_u[:, :, :, 3 - shift_by : 3 - shift_by + cols_z].astype(jnp.float32)
         total = total + weight_now * (ahead_w - behind_w) - weight_now * (ahead_u - behind_u)
     flat = total.astype(jnp.bfloat16).reshape(snaps, planes * cols_x * cols_z)
-    local_gram = lax.dot_general(
-        flat, flat, (((1,), (1,)), ((), ())), preferred_element_type=jnp.float32
-    )
-    gram = lax.psum(local_gram, ("gx", "gz"))
     count_x = lax.axis_size("gx")
     count_z = lax.axis_size("gz")
     total_x = cols_x * count_x
     total_z = cols_z * count_z
+    position = local_position(anchor_index, planes, cols_x, cols_z, total_x, total_z)
+    cell_of = lax.broadcasted_iota(jnp.int32, (kept, planes * cols_x * cols_z), 1)
+    chosen = (cell_of == position[:, None]).astype(jnp.bfloat16)
+    local = lax.dot_general(
+        jnp.concatenate([flat, chosen], axis=0),
+        flat,
+        (((1,), (1,)), ((), ())),
+        preferred_element_type=jnp.float32,
+    )
+    gram, picked = total_of(local, snaps, kept)
     gram = gram / float(planes * total_x * total_z)
     scale = jnp.where(snapshot_rank < kept, 1.0, 0.25).astype(jnp.float32)
     weighted = scale[:, None] * gram * scale[None, :]
@@ -62,17 +94,7 @@
         basis_now = orthonormal(jnp.dot(weighted, basis_now, precision=lax.Precision.HIGHEST))
     coef = (scale[:, None] * basis_now).astype(jnp.bfloat16)
     raw = lax.dot_general(coef, flat, (((0,), (0,)), ((), ())), preferred_element_type=jnp.float32)
-    plane_of = anchor_index // (total_x * total_z)
-    remain = anchor_index % (total_x * total_z)
-    local_x = remain // total_z - lax.axis_index("gx") * cols_x
-    local_z = remain % total_z - lax.axis_index("gz") * cols_z
-    owned = (local_x >= 0) & (local_x < cols_x) & (local_z >= 0) & (local_z < cols_z)
-    position = (plane_of * cols_x + jnp.clip(local_x, 0, cols_x - 1)) * cols_z + jnp.clip(
-        local_z, 0, cols_z - 1
-    )
-    values = jnp.take_along_axis(raw, position[:, None], axis=1)[:, 0]
-    term = jnp.where(owned, values, 0.0)
-    anchor = lax.psum(term, ("gx", "gz"))
+    anchor = jnp.sum(picked * coef.T.astype(jnp.float32), axis=1)
     orient = anchor / jnp.maximum(jnp.abs(anchor), 1.0)
     modes = (raw * orient[:, None]).astype(jnp.bfloat16).reshape(kept, planes, cols_x, cols_z)
     return (modes, basis_now * orient[None, :])

time: 661 us -> 138 us (0.21)
  waiting for transfers between devices: 449 us -> 14.2 us
  blocking collectives: 108 us -> 34.1 us
  between operations: 14.4 us -> 1.01 us
    psum x1 -> x0, waiting for transfers between devices: 445 us -> none  [body(): gram = lax.psum(local_gram, ('gx', 'gz'))]
    psum x1 -> x0, blocking collectives: 108 us -> none  [body(): anchor = lax.psum(term, ('gx', 'gz'))]
    all_to_all x0 -> x2, blocking collectives: none -> 34.1 us  [exchanged(): return lax.all_to_all(rows, axis, 0, 0, tiled=True)]
    all_to_all x0 -> x1, waiting for transfers between devices: none -> 10.7 us  [exchanged(): return lax.all_to_all(rows, axis, 0, 0, tiled=True)]
  transfers between devices with their start and end apart: 5 -> 5, of which waited for: 2 -> 2; matrix products, arithmetic and copies ran while one was open for 0% -> 2% of each run, Pallas kernels for 0% -> 0%
where the time goes in v1:
time: 138 us
  other arithmetic  46.1 us (33%)
  blocking collectives  34.1 us (25%)
  starting transfers between devices  28.5 us (21%)
  waiting for transfers between devices  14.2 us (10%)
  local copies, waits for them, and re-layouts  9.87 us (7%)
  matrix products  4.05 us (3%)
    all_to_all x2, blocking collectives, exchanged(): return lax.all_to_all(rows, axis, 0, 0, tiled=True)  34.1 us
    another operation x9, other arithmetic, orthonormal(): lower = jnp.linalg.cholesky(inner)  19.6 us
    ppermute x2, starting transfers between devices, extended(): lax.ppermute(head, axis, [((i + 1) % count, i) for i in range(count)])  18.8 us
    another operation x6, other arithmetic, orthonormal(): return jax.scipy.linalg.solve_triangular(lower, block.T, lower=True).T  16.6 us
    all_to_all x1, waiting for transfers between devices, exchanged(): return lax.all_to_all(rows, axis, 0, 0, tiled=True)  10.7 us
    convert_element_type x1, other arithmetic, body(): flat = total.astype(jnp.bfloat16).reshape(snaps, planes * cols_x * cols_z)  8.57 us
    all_to_all x1, starting transfers between devices, exchanged(): return lax.all_to_all(rows, axis, 0, 0, tiled=True)  5.88 us
    unnamed x14, local copies, waits for them, and re-layouts  4.38 us
  transfers between devices with their start and end apart: 5, of which 2 were waited for; matrix products, arithmetic and copies ran while one was open for 2% of the time, Pallas kernels for 0%

profile of v1, /device:TPU:1, one launch (start us, length us, event | category | flops | bytes accessed | tf_op | source)
XLA Modules:
  0.0 137.8 jit_solution(3801280896518517126)
XLA Ops:
  0.6 3.6 %fusion.44 = (bf16[1,128,2,24,128]{4,3,2,1,0:T(8,128)(2,1)}, bf16[1,128,2,24,128]{4,3,2,1,0:T(8,128)(2,1)S(1)}) fusion(bf16[2,128,2,24,128]{4,3,2,1,0:T(8,128)(2,1)} %param.7), kind=kLoop, calls=%fused_computation.86 | loop fusion | bytes 6291456 | tf_op jit(solution)/shard_map/slice | solution.py:64
  4.2 1.1 copy.36
  5.4 0.8 fusion.45
  6.1 12.4 %collective-permute-start = (bf16[128,2,3,128]{0,3,2,1:T(8,128)(2,1)}, bf16[128,2,3,128]{0,3,2,1:T(8,128)(2,1)S(1)}, u32[]{:S(2)}, u32[]{:S(2)}) collective-permute-start(bf16[128,2,3,128]{0,3,2,1:T(8,128)(2,1)} %get-tuple-element.6), channel_id=1, source_target_pairs={{12,0},{24,12},{36,24},{48,36},{60,48},{72,60},{84,72},{96,84},{10... | collective-permute-start | bytes 589832 | tf_op jit(solution)/shard_map/ppermute | solution.py:18
  18.5 1.9 %collective-permute-start.1 = (bf16[128,2,3,128]{0,3,2,1:T(8,128)(2,1)}, bf16[128,2,3,128]{0,3,2,1:T(8,128)(2,1)}, u32[]{:S(2)}, u32[]{:S(2)}) collective-permute-start(bf16[128,2,3,128]{0,3,2,1:T(8,128)(2,1)} %get-tuple-element.7), channel_id=1, source_target_pairs={{0,12},{12,24},{24,36},{36,48},{48,60},{60,72},{72,84},{84,96},{96... | collective-permute-start | bytes 589832 | tf_op jit(solution)/shard_map/ppermute | solution.py:16
  20.5 2.1 %copy.37 = bf16[1,128,2,24,128]{1,4,3,2,0:T(8,128)(2,1)S(1)} copy(bf16[1,128,2,24,128]{4,3,2,1,0:T(8,128)(2,1)} %get-tuple-element.4) | data formatting | bytes 3145728
  22.7 6.4 %collective-permute-start.2 = (bf16[128,2,24,3]{0,2,3,1:T(8,128)(2,1)S(1)}, bf16[128,2,24,3]{0,2,3,1:T(8,128)(2,1)S(1)}, u32[]{:S(2)}, u32[]{:S(2)}) collective-permute-start(bf16[128,2,24,3]{0,2,3,1:T(8,128)(2,1)S(1)} %copy.27), channel_id=1, source_target_pairs={{1,0},{2,1},{3,2},{4,3},{5,4},{6,5},{7,6},{8,7},{9,8},{10,9},{11,1... | collective-permute-start | bytes 110600 | tf_op jit(solution)/shard_map/ppermute | solution.py:18
  29.1 1.9 %collective-permute-start.3 = (bf16[128,2,24,3]{0,2,3,1:T(8,128)(2,1)S(1)}, bf16[128,2,24,3]{0,2,3,1:T(8,128)(2,1)S(1)}, u32[]{:S(2)}, u32[]{:S(2)}) collective-permute-start(bf16[128,2,24,3]{0,2,3,1:T(8,128)(2,1)S(1)} %copy.29), channel_id=1, source_target_pairs={{0,1},{1,2},{2,3},{3,4},{4,5},{5,6},{6,7},{7,8},{8,9},{9,10},{10,1... | collective-permute-start | bytes 110600 | tf_op jit(solution)/shard_map/ppermute | solution.py:16
  31.5 3.5 %collective-permute-done.3 = bf16[128,2,24,3]{0,2,3,1:T(8,128)(2,1)S(1)} collective-permute-done((bf16[128,2,24,3]{0,2,3,1:T(8,128)(2,1)S(1)}, bf16[128,2,24,3]{0,2,3,1:T(8,128)(2,1)S(1)}, u32[]{:S(2)}, u32[]{:S(2)}) %collective-permute-start.3) | collective-permute-done | bytes 36896 | tf_op jit(solution)/shard_map/ppermute | solution.py:16
  35.0 8.6 %subtract_convert_fusion = bf16[128,2,24,128]{0,3,2,1:T(8,128)(2,1)S(1)} fusion(bf16[128,2,24,128]{0,3,2,1:T(8,128)(2,1)S(1)} %bitcast.66, bf16[128,2,24,3]{0,3,2,1:T(4,128)(2,1)S(1)} %copy.30, bf16[128,2,24,3]{0,3,2,1:T(4,128)(2,1)S(1)} %copy.28, bf16[128,2,3,128]{0,3,2,1:T(8,128)(2,1)} %collective-permute-done.1, ...), kind=kLoop, calls=%fused_computation.7 | loop fusion | flops 51904512 | bytes 5185536 | tf_op jit(solution)/shard_map/convert_element_type | solution.py:74
  43.6 1.0 fusion.1
  44.9 22.5 %all_to_all.24 = f32[64,1,384]{2,1,0:T(1,128)S(1)} all-to-all(f32[64,1,384]{2,1,0:T(1,128)S(1)} %copy.31), channel_id=1, replica_groups=mesh['gx'=64,'gz'=12] {'gx'}, dimensions={0} | all-to-all | bytes 196608 | tf_op jit(solution)/shard_map/all_to_all | solution.py:41
  67.6 11.6 %all_to_all.25 = f32[12,1,384]{2,1,0:T(1,128)S(1)} all-to-all(f32[12,1,384]{2,1,0:T(1,128)S(1)} %broadcast_in_dim.25), channel_id=1, replica_groups=mesh['gx'=64,'gz'=12] {'gz'}, dimensions={0} | all-to-all | bytes 36864 | tf_op jit(solution)/shard_map/all_to_all | solution.py:41
  79.2 0.7 broadcast_in_dim.26
  79.9 5.9 %all-to-all-start.2 = ((f32[64,1,384]{2,1,0:T(1,128)}), f32[64,1,384]{2,1,0:T(1,128)S(1)}, u32[]{:S(2)}, u32[]{:S(2)}) async-start(f32[64,1,384]{2,1,0:T(1,128)} %broadcast_in_dim.26), calls=%async_computation.2 | async-start | bytes 196608 | tf_op jit(solution)/shard_map/all_to_all | solution.py:41
  85.8 10.7 %all-to-all-done.2 = f32[64,1,384]{2,1,0:T(1,128)S(1)} async-done(((f32[64,1,384]{2,1,0:T(1,128)}), f32[64,1,384]{2,1,0:T(1,128)S(1)}, u32[]{:S(2)}, u32[]{:S(2)}) %all-to-all-start.2) | async-done | bytes 98336 | tf_op jit(solution)/shard_map/all_to_all | solution.py:41
  97.1 5.8 %cholesky.59 = f32[64,64]{1,0:T(8,128)S(1)} custom-call(f32[64,64]{1,0:T(8,128)S(1)} %fusion.31), custom_call_target="Cholesky" | custom-call | tf_op jit(solution)/shard_map/jit(cholesky)/cholesky | solution.py:27
  104.3 4.9 %custom-call.7 = f32[1,64,64]{1,2,0:T(8,128)S(1)} custom-call(f32[1,64,64]{2,1,0:T(8,128)S(1)} %fusion.16), custom_call_target="InvertDiagBlocksLowerTriangular" | custom-call | tf_op jit(solution)/shard_map/jit(_solve_triangular)/triangular_solve | solution.py:28
  110.1 5.8 %cholesky.70 = f32[64,64]{1,0:T(8,128)S(1)} custom-call(f32[64,64]{1,0:T(8,128)S(1)} %fusion.27), custom_call_target="Cholesky" | custom-call | tf_op jit(solution)/shard_map/jit(cholesky)/cholesky | solution.py:27
  117.2 4.9 %custom-call.8 = f32[1,64,64]{1,2,0:T(8,128)S(1)} custom-call(f32[1,64,64]{2,1,0:T(8,128)S(1)} %fusion.17), custom_call_target="InvertDiagBlocksLowerTriangular" | custom-call | tf_op jit(solution)/shard_map/jit(_solve_triangular)/triangular_solve | solution.py:28
  123.0 5.8 %cholesky.81 = f32[64,64]{1,0:T(8,128)S(1)} custom-call(f32[64,64]{1,0:T(8,128)S(1)} %fusion.23), custom_call_target="Cholesky" | custom-call | tf_op jit(solution)/shard_map/jit(cholesky)/cholesky | solution.py:27
  130.2 4.9 %custom-call.9 = f32[1,64,64]{1,2,0:T(8,128)S(1)} custom-call(f32[1,64,64]{2,1,0:T(8,128)S(1)} %fusion.18), custom_call_target="InvertDiagBlocksLowerTriangular" | custom-call | tf_op jit(solution)/shard_map/jit(_solve_triangular)/triangular_solve | solution.py:28
  135.5 0.7 multiply_bitcast_fusion
  136.8 1.0 copy.38
  (55 shorter events, 8.2 us)
Async XLA Ops:
  0.6 95.9 %copy-start = (f32[128,64]{0,1:T(8,128)S(1)}, f32[128,64]{0,1:T(8,128)}, u32[]{:S(2)}) copy-start(f32[128,64]{0,1:T(8,128)} %param.10) | copy-start | bytes 98308
  4.2 26.8 %copy-start.3 = (s32[64]{0:T(128)S(1)}, s32[64]{0:T(128)}, u32[]{:S(2)}) copy-start(s32[64]{0:T(128)} %param.9) | copy-start | bytes 772
  6.1 28.9 %collective-permute-start = (bf16[128,2,3,128]{0,3,2,1:T(8,128)(2,1)}, bf16[128,2,3,128]{0,3,2,1:T(8,128)(2,1)S(1)}, u32[]{:S(2)}, u32[]{:S(2)}) collective-permute-start(bf16[128,2,3,128]{0,3,2,1:T(8,128)(2,1)} %get-tuple-element.6), channel_id=1, source_target_pairs={{12,0},{24,12},{36,24},{48,36},{60,48},{72,60},{84,72},{96,84},{10... | collective-permute-start | bytes 589832 | tf_op jit(solution)/shard_map/ppermute | solution.py:18
  18.5 16.5 %collective-permute-start.1 = (bf16[128,2,3,128]{0,3,2,1:T(8,128)(2,1)}, bf16[128,2,3,128]{0,3,2,1:T(8,128)(2,1)}, u32[]{:S(2)}, u32[]{:S(2)}) collective-permute-start(bf16[128,2,3,128]{0,3,2,1:T(8,128)(2,1)} %get-tuple-element.7), channel_id=1, source_target_pairs={{0,12},{12,24},{24,36},{36,48},{48,60},{60,72},{72,84},{84,96},{96... | collective-permute-start | bytes 589832 | tf_op jit(solution)/shard_map/ppermute | solution.py:16
  22.7 8.8 %collective-permute-start.2 = (bf16[128,2,24,3]{0,2,3,1:T(8,128)(2,1)S(1)}, bf16[128,2,24,3]{0,2,3,1:T(8,128)(2,1)S(1)}, u32[]{:S(2)}, u32[]{:S(2)}) collective-permute-start(bf16[128,2,24,3]{0,2,3,1:T(8,128)(2,1)S(1)} %copy.27), channel_id=1, source_target_pairs={{1,0},{2,1},{3,2},{4,3},{5,4},{6,5},{7,6},{8,7},{9,8},{10,9},{11,1... | collective-permute-start | bytes 110600 | tf_op jit(solution)/shard_map/ppermute | solution.py:18
  29.1 5.9 %collective-permute-start.3 = (bf16[128,2,24,3]{0,2,3,1:T(8,128)(2,1)S(1)}, bf16[128,2,24,3]{0,2,3,1:T(8,128)(2,1)S(1)}, u32[]{:S(2)}, u32[]{:S(2)}) collective-permute-start(bf16[128,2,24,3]{0,2,3,1:T(8,128)(2,1)S(1)} %copy.29), channel_id=1, source_target_pairs={{0,1},{1,2},{2,3},{3,4},{4,5},{5,6},{6,7},{7,8},{8,9},{9,10},{10,1... | collective-permute-start | bytes 110600 | tf_op jit(solution)/shard_map/ppermute | solution.py:16
  43.6 1.2 copy-start.1
  43.6 42.1 %copy-start.4 = (s32[128]{0:T(128)S(1)}, s32[128]{0:T(128)}, u32[]{:S(2)}) copy-start(s32[128]{0:T(128)} %param.8) | copy-start | bytes 1540
  44.8 91.4 %copy-start.2 = (bf16[128,2,24,128]{0,3,2,1:T(8,128)(2,1)S(1)}, bf16[128,2,24,128]{0,3,2,1:T(8,128)(2,1)}, u32[]{:S(2)}) copy-start(bf16[128,2,24,128]{0,3,2,1:T(8,128)(2,1)} %copy-done.1) | copy-start | bytes 4718596
  79.9 16.6 %all-to-all-start.2 = ((f32[64,1,384]{2,1,0:T(1,128)}), f32[64,1,384]{2,1,0:T(1,128)S(1)}, u32[]{:S(2)}, u32[]{:S(2)}) async-start(f32[64,1,384]{2,1,0:T(1,128)} %broadcast_in_dim.26), calls=%async_computation.2 | async-start | bytes 196608 | tf_op jit(solution)/shard_map/all_to_all | solution.py:41

commit v2 on v0

v2 whole, which is shorter than its diff:
```python
from functools import partial

import jax
import jax.numpy as jnp
import numpy as np
from jax import lax
from jax.experimental import pallas as pl
from jax.experimental.pallas import tpu as pltpu
from jax.sharding import PartitionSpec as P

ITERS = 3
REACH = 3
TAPS = (45.0, -9.0, 1.0)
TAP_SUM = 60.0
GROUP = 8
HIGHEST = lax.Precision.HIGHEST
NT = (((1,), (1,)), ((), ()))
TN = (((0,), (0,)), ((), ()))


def tap(offset):
    size = abs(offset)
    if size < 1 or size > REACH:
        return 0.0
    return TAPS[size - 1] if offset > 0 else -TAPS[size - 1]


def band(points, first, count):
    return np.array([[tap(first + j - i) for j in range(count)] for i in range(points)], np.float32)


def tables(planes, cols_x, cols_z):
    lines = planes * cols_x
    eye = np.eye(GROUP, dtype=np.float32)
    order = np.einsum("ab,mn->ambn", np.eye(lines, dtype=np.float32), eye)
    order = order.transpose(0, 1, 3, 2).reshape(lines * GROUP, GROUP * lines)
    along_x = np.kron(np.eye(planes, dtype=np.float32), band(cols_x, 0, cols_x))
    along_x = np.einsum("ab,mn->ambn", along_x, eye).transpose(0, 1, 3, 2)
    along_x = along_x.reshape(lines * GROUP, GROUP * lines)
    along_z = -band(cols_z, 0, cols_z).T
    edge_z = np.zeros((2 * GROUP, cols_z), np.float32)
    edge_z[:REACH] = -band(cols_z, cols_z, REACH).T
    edge_z[GROUP : GROUP + REACH] = -band(cols_z, -REACH, REACH).T
    ends_z = np.zeros((2 * GROUP, cols_z), np.float32)
    ends_x = np.zeros((2, REACH, planes, GROUP, GROUP, planes, cols_x), np.float32)
    for h in range(REACH):
        ends_z[h, h] = 1.0
        ends_z[GROUP + h, cols_z - REACH + h] = 1.0
        for p in range(planes):
            for m in range(GROUP):
                ends_x[0, h, p, m, m, p, h] = 1.0
                ends_x[1, h, p, m, m, p, cols_x - REACH + h] = 1.0
    ends_x = ends_x.reshape(2 * REACH * planes * GROUP, GROUP * lines)
    cast = lambda table: jnp.asarray(table, jnp.bfloat16)
    return {
        "order": cast(order),
        "order_t": cast(order.T),
        "along_x": cast(along_x),
        "along_z": cast(along_z),
        "edge_z": cast(edge_z),
        "ends_z": cast(ends_z),
        "ends_x": cast(ends_x),
    }


def matmul(left, right, dims=None):
    dims = dims or (((1,), (0,)), ((), ()))
    return lax.dot_general(left, right, dims, preferred_element_type=jnp.float32)


def flat_group(ref, field, group):
    block = ref[field, pl.ds(group * GROUP, GROUP)]
    return block.reshape(-1, block.shape[-1])


def ends_kernel(velocity, ends_x, ends_z, order_t, head_w, tail_w, head_u, tail_u):
    planes = velocity.shape[2]
    for q in range(velocity.shape[1] // GROUP):
        rows = matmul(ends_x[...], flat_group(velocity, 1, q)).astype(jnp.bfloat16)
        here = pl.ds(q * GROUP, GROUP)
        for h in range(REACH):
            for p in range(planes):
                at = (h * planes + p) * GROUP
                head_w[h, p, here, :] = rows[at : at + GROUP]
                at = at + REACH * planes * GROUP
                tail_w[h, p, here, :] = rows[at : at + GROUP]
        cols = matmul(ends_z[...], flat_group(velocity, 0, q), NT).astype(jnp.bfloat16)
        cols = matmul(cols, order_t[...]).astype(jnp.bfloat16)
        head_u[here, :] = cols[:GROUP]
        tail_u[here, :] = cols[GROUP:]


def inner_kernel(velocity, along_x, along_z, order, out):
    lines = out.shape[0]
    cols_z = out.shape[2]
    for q in range(0, velocity.shape[1] // GROUP, 2):
        w_two = jnp.concatenate([flat_group(velocity, 1, q), flat_group(velocity, 1, q + 1)], axis=1)
        u_two = jnp.concatenate([flat_group(velocity, 0, q), flat_group(velocity, 0, q + 1)], axis=1)
        part = matmul(along_x[...], w_two)
        moved = matmul(order[...], u_two).astype(jnp.bfloat16)
        for half in range(2):
            lanes = slice(half * cols_z, (half + 1) * cols_z)
            value = part[:, lanes] + matmul(moved[:, lanes], along_z[...])
            out[:, pl.ds((q + half) * GROUP, GROUP), :] = value.reshape(lines, GROUP, cols_z)


def gram_kernel(planes, cols_x, inner, left_w, right_w, left_u, right_u, edge_z, place, vort, rows_out, work):
    lines, snaps, cols_z = inner.shape
    kept = place.shape[0]
    for q in range(snaps // GROUP):
        here = pl.ds(q * GROUP, GROUP)
        cols = jnp.concatenate([right_u[here, :], left_u[here, :]], axis=0)
        value = matmul(cols, edge_z[...], TN).reshape(lines, GROUP, cols_z)
        work[:, here, :] = inner[:, here, :] + value
    gram = jnp.zeros((snaps + kept, snaps), jnp.float32)
    lane = lax.broadcasted_iota(jnp.int32, (kept, 2 * cols_z), 1)
    for pair in range(lines // 2):
        sides = []
        for line in (2 * pair, 2 * pair + 1):
            p, x = line // cols_x, line % cols_x
            value = work[line]
            for h in range(REACH):
                if tap(cols_x + h - x):
                    value = value + tap(cols_x + h - x) * right_w[h, p].astype(jnp.float32)
                if tap(h - REACH - x):
                    value = value + tap(h - REACH - x) * left_w[h, p].astype(jnp.float32)
            value = (value * (1.0 / TAP_SUM)).astype(jnp.bfloat16)
            vort[line] = value
            sides.append(value)
        both = jnp.concatenate(sides, axis=1)
        chosen = jnp.where(lane == place[...] - 2 * pair * cols_z, 1.0, 0.0).astype(jnp.bfloat16)
        gram = gram + matmul(jnp.concatenate([both, chosen], axis=0), both, NT)
    for part in range((snaps + kept) // kept):
        rows_out[:, part * snaps : (part + 1) * snaps] = gram[part * kept : (part + 1) * kept]


def inverse_root(value):
    root = lax.rsqrt(value)
    return root * (1.5 - 0.5 * value * root * root)


def orthonormal_rows(block, inner):
    kept, snaps = block.shape
    tile = (GROUP, snaps)
    count = kept // GROUP
    row_at = lax.broadcasted_iota(jnp.int32, tile, 0)
    inner_rows = [inner[GROUP * i : GROUP * (i + 1)] for i in range(count)]
    block_rows = [block[GROUP * i : GROUP * (i + 1)] for i in range(count)]
    for b in range(count):
        first = GROUP * b
        cols = [
            [jnp.broadcast_to(inner_rows[r][:, first + t : first + t + 1], tile) for r in range(b, count)]
            for t in range(GROUP)
        ]
        for t in range(GROUP):
            root = inverse_root(jnp.broadcast_to(cols[t][0][t : t + 1], tile))
            factor = [col * root for col in cols[t]]
            below = jnp.where(row_at > t, factor[0], 0.0)
            inner_row = jnp.broadcast_to(inner_rows[b][t : t + 1], (GROUP, kept)) * root[:, :kept]
            block_row = jnp.broadcast_to(block_rows[b][t : t + 1], tile) * root
            for later in range(t + 1, GROUP):
                share = jnp.broadcast_to(factor[0][later : later + 1], tile)
                cols[later] = [col - part * share for col, part in zip(cols[later], factor)]
            inner_rows[b] = inner_rows[b] - below[:, :kept] * inner_row
            block_rows[b] = jnp.where(row_at == t, block_row, block_rows[b] - below * block_row)
            for r in range(b + 1, count):
                inner_rows[r] = inner_rows[r] - factor[r - b][:, :kept] * inner_row
                block_rows[r] = block_rows[r] - factor[r - b] * block_row
    return jnp.concatenate(block_rows, axis=0)


def modes_kernel(cells, rows, rank, start, vort, modes, basis, work):
    kept, snaps = start.shape
    lines = vort.shape[0]
    gram = jnp.concatenate(
        [rows[:, b * snaps : (b + 1) * snaps] for b in range(snaps // kept)], axis=0
    ) * (1.0 / cells)
    picked = rows[:, snaps // kept * snaps :]
    scale = jnp.where(rank[...] < kept, 1.0, 0.25).astype(jnp.float32)
    now = start[...]
    for step in range(ITERS):
        block = lax.dot_general(now * scale, gram, NT, precision=HIGHEST, preferred_element_type=jnp.float32)
        block = block * scale
        inner = lax.dot_general(block, block, NT, precision=HIGHEST, preferred_element_type=jnp.float32)
        now = orthonormal_rows(block, inner)
    coef = (now * scale).astype(jnp.bfloat16)
    anchor = jnp.sum(picked * coef.astype(jnp.float32), axis=1, keepdims=True)
    orient = anchor / jnp.maximum(jnp.abs(anchor), 1.0)
    basis[...] = now * orient
    for line in range(lines):
        work[pl.ds(line, kept, stride=lines), :] = matmul(coef, vort[line]) * orient
    modes[...] = work[...].astype(jnp.bfloat16).reshape(modes.shape)


def local_place(anchor_index, planes, cols_x, cols_z, total_x, total_z):
    plane_of = anchor_index // (total_x * total_z)
    remain = anchor_index % (total_x * total_z)
    local_x = remain // total_z - lax.axis_index("gx") * cols_x
    local_z = remain % total_z - lax.axis_index("gz") * cols_z
    owned = (local_x >= 0) & (local_x < cols_x) & (local_z >= 0) & (local_z < cols_z)
    return jnp.where(owned, (plane_of * cols_x + local_x) * cols_z + local_z, -1)


def shifted(value, axis, step):
    count = lax.axis_size(axis)
    return lax.ppermute(value, axis, [(i, (i + step) % count) for i in range(count)])


def exchanged(rows, axis):
    return lax.all_to_all(rows, axis, 0, 0, tiled=True)


def summed(rows, axis):
    count = lax.axis_size(axis)
    return jnp.sum(rows.reshape((count, rows.shape[0] // count) + rows.shape[1:]), axis=0)


def copies(rows, axis):
    return jnp.tile(rows, (lax.axis_size(axis), 1))


def body(velocity, snapshot_rank, anchor_index, start_basis):
    _, snaps, planes, cols_x, cols_z = velocity.shape
    kept = start_basis.shape[1]
    lines = planes * cols_x
    total_x = cols_x * lax.axis_size("gx")
    total_z = cols_z * lax.axis_size("gz")
    table = tables(planes, cols_x, cols_z)
    steps = 4
    share = snaps // steps
    whole = lambda array: pl.BlockSpec(array.shape, lambda i: (0,) * array.ndim)
    velocity_spec = pl.BlockSpec((2, share, planes, cols_x, cols_z), lambda i: (0, i, 0, 0, 0))
    shape = jax.ShapeDtypeStruct
    side_w = pl.BlockSpec((REACH, planes, share, cols_z), lambda i: (0, 0, i, 0))
    side_u = pl.BlockSpec((share, lines * GROUP), lambda i: (i, 0))
    given = [table["ends_x"], table["ends_z"], table["order_t"]]
    head_w, tail_w, head_u, tail_u = pl.pallas_call(
        ends_kernel,
        grid=(steps,),
        in_specs=[velocity_spec] + [whole(t) for t in given],
        out_specs=[side_w, side_w, side_u, side_u],
        out_shape=[shape((REACH, planes, snaps, cols_z), jnp.bfloat16)] * 2
        + [shape((snaps, lines * GROUP), jnp.bfloat16)] * 2,
        name="ends",
    )(velocity, *given)
    left_w = shifted(tail_w, "gx", 1)
    right_w = shifted(head_w, "gx", -1)
    left_u = shifted(tail_u, "gz", 1)
    right_u = shifted(head_u, "gz", -1)
    given = [table["along_x"], table["along_z"], table["order"]]
    inner = pl.pallas_call(
        inner_kernel,
        grid=(steps,),
        in_specs=[velocity_spec] + [whole(t) for t in given],
        out_specs=pl.BlockSpec((lines, share, cols_z), lambda i: (0, i, 0)),
        out_shape=shape((lines, snaps, cols_z), jnp.float32),
        name="inner",
    )(velocity, *given)
    place = local_place(anchor_index, planes, cols_x, cols_z, total_x, total_z)
    vort, rows = pl.pallas_call(
        partial(gram_kernel, planes, cols_x),
        out_shape=[
            shape((lines, snaps, cols_z), jnp.bfloat16),
            shape((kept, (snaps // kept + 1) * snaps), jnp.float32),
        ],
        scratch_shapes=[pltpu.VMEM((lines, snaps, cols_z), jnp.float32)],
        name="gram",
    )(inner, left_w, right_w, left_u, right_u, table["edge_z"], place[:, None])
    mine = summed(exchanged(rows, "gx"), "gx")
    mine = summed(exchanged(copies(mine, "gz"), "gz"), "gz")
    rows = exchanged(copies(mine, "gx"), "gx")
    modes, basis = pl.pallas_call(
        partial(modes_kernel, float(planes * total_x * total_z)),
        out_shape=[
            shape((kept, planes, cols_x, cols_z), jnp.bfloat16),
            shape((kept, snaps), jnp.float32),
        ],
        scratch_shapes=[pltpu.VMEM((kept * lines, cols_z), jnp.float32)],
        name="modes",
    )(rows, snapshot_rank[None, :], start_basis.T, vort)
    return modes, basis.T


def solution(mesh):
    return jax.shard_map(
        body,
        mesh=mesh,
        in_specs=(P(None, None, None, "gx", "gz"), P(), P(), P()),
        out_specs=(P(None, None, "gx", "gz"), P()),
        check_vma=False,
    )
```

time: 661 us -> 107 us (0.16)
  waiting for transfers between devices: 449 us -> 0.01 us
  blocking collectives: 108 us -> 50.8 us
  other arithmetic: 49.9 us -> 0.16 us
  Pallas kernels: 0 us -> 28.1 us
  between operations: 14.4 us -> 0.74 us
  matrix products: 6.66 us -> 0 us
    psum x1 -> x0, waiting for transfers between devices: 445 us -> none  [body(): gram = lax.psum(local_gram, ('gx', 'gz'))]
    psum x1 -> x0, blocking collectives: 108 us -> none  [body(): anchor = lax.psum(term, ('gx', 'gz'))]
    all_to_all x0 -> x3, blocking collectives: none -> 50.8 us  [exchanged(): return lax.all_to_all(rows, axis, 0, 0, tiled=True)]
    another operation x15 -> x0, other arithmetic: 36.2 us -> none  [the longest x9 19.6 us: orthonormal(): lower = jnp.linalg.cholesky(inner)]
    pallas_call x0 -> x4, Pallas kernels: none -> 28.1 us  [the longest x1 11.2 us: body(): pl.pallas_call(partial(modes_kernel, float(planes * total_x * total_z)),...]
    convert_element_type x1 -> x0, other arithmetic: 12.7 us -> none  [body(): flat = total.astype(jnp.bfloat16).reshape(snaps, planes * cols_x * cols_z)]
  transfers between devices with their start and end apart: 5 -> 4, of which waited for: 2 -> 0; matrix products, arithmetic and copies ran while one was open for 0% -> 1% of each run, Pallas kernels for 0% -> 6%
where the time goes in v2:
time: 107 us
  blocking collectives  50.8 us (47%)
  Pallas kernels  28.1 us (26%)
  starting transfers between devices  22.9 us (21%)
  local copies, waits for them, and re-layouts  3.83 us (4%)
    all_to_all x3, blocking collectives, exchanged(): return lax.all_to_all(rows, axis, 0, 0, tiled=True)  50.8 us
    ppermute x4, starting transfers between devices, shifted(): lax.ppermute(value, axis, [(i, (i + step) % count) for i in range(count)])  22.9 us
    pallas_call x1, Pallas kernels, body(): pl.pallas_call(partial(modes_kernel, float(planes * total_x * total_z)),...  11.2 us
    pallas_call x1, Pallas kernels, body(): pl.pallas_call(inner_kernel, grid=(steps,), in_specs=[velocity_spec] + [w...  6.19 us
    pallas_call x1, Pallas kernels, body(): pl.pallas_call(ends_kernel, grid=(steps,), in_specs=[velocity_spec] + [wh...  5.86 us
    pallas_call x1, Pallas kernels, body(): pl.pallas_call(partial(gram_kernel, planes, cols_x), out_shape=[shape((li...  4.8 us
  transfers between devices with their start and end apart: 4, of which 0 were waited for; matrix products, arithmetic and copies ran while one was open for 1% of the time, Pallas kernels for 6%

profile of v2, /device:TPU:1, one launch (start us, length us, event | category | flops | bytes accessed | tf_op | source)
XLA Modules:
  0.0 106.6 jit_solution(1439028159080653385)
XLA Ops:
  0.6 5.9 %ends.1 = (bf16[3,2,128,128]{3,2,1,0:T(8,128)(2,1)}, bf16[3,2,128,128]{3,2,1,0:T(8,128)(2,1)}, bf16[128,384]{1,0:T(8,128)(2,1)}, bf16[128,384]{1,0:T(8,128)(2,1)}) custom-call(bf16[2,128,2,24,128]{4,3,2,1,0:T(8,128)(2,1)} %velocity.3, bf16[96,384]{1,0:T(8,128)(2,1)} %constant.68.clone.ends_x, bf16[16,128]{1,0:T(8,128)(2,1)} %constant.67.clone.ends_z, ...), custom_call_target="tpu_custom_call" | custom-call | tf_op jit(solution)/shard_map/ends/pallas_call | solution.py:237
  6.5 4.8 %collective-permute-start.2 = (bf16[128,384]{1,0:T(8,128)(2,1)}, bf16[128,384]{1,0:T(8,128)(2,1)S(1)}, u32[]{:S(2)}, u32[]{:S(2)}) collective-permute-start(bf16[128,384]{1,0:T(8,128)(2,1)} %get-tuple-element.12), channel_id=1, source_target_pairs={{0,1},{1,2},{2,3},{3,4},{4,5},{5,6},{6,7},{7,8},{8,9},{9,10},{10,1... | collective-permute-start | bytes 294920 | tf_op jit(solution)/shard_map/ppermute | solution.py:206
  11.3 12.2 %collective-permute-start.3 = (bf16[128,384]{1,0:T(8,128)(2,1)}, bf16[128,384]{1,0:T(8,128)(2,1)S(1)}, u32[]{:S(2)}, u32[]{:S(2)}) collective-permute-start(bf16[128,384]{1,0:T(8,128)(2,1)} %get-tuple-element.13), channel_id=1, source_target_pairs={{0,11},{1,0},{2,1},{3,2},{4,3},{5,4},{6,5},{7,6},{8,7},{9,8},{10,9... | collective-permute-start | bytes 294920 | tf_op jit(solution)/shard_map/ppermute | solution.py:206
  23.6 4.0 %collective-permute-start = (bf16[3,2,128,128]{3,2,1,0:T(8,128)(2,1)}, bf16[3,2,128,128]{3,2,1,0:T(8,128)(2,1)S(1)}, u32[]{:S(2)}, u32[]{:S(2)}) collective-permute-start(bf16[3,2,128,128]{3,2,1,0:T(8,128)(2,1)} %get-tuple-element.10), channel_id=1, source_target_pairs={{0,12},{12,24},{24,36},{36,48},{48,60},{60,72},{72,84},{84,96},{96... | collective-permute-start | bytes 589832 | tf_op jit(solution)/shard_map/ppermute | solution.py:206
  27.5 1.9 %collective-permute-start.1 = (bf16[3,2,128,128]{3,2,1,0:T(8,128)(2,1)}, bf16[3,2,128,128]{3,2,1,0:T(8,128)(2,1)S(1)}, u32[]{:S(2)}, u32[]{:S(2)}) collective-permute-start(bf16[3,2,128,128]{3,2,1,0:T(8,128)(2,1)} %get-tuple-element.11), channel_id=1, source_target_pairs={{0,756},{12,0},{24,12},{36,24},{48,36},{60,48},{72,60},{84,72},{96... | collective-permute-start | bytes 589832 | tf_op jit(solution)/shard_map/ppermute | solution.py:206
  29.5 0.7 copy.16.place
  30.2 6.2 %inner.1 = f32[48,128,128]{2,1,0:T(8,128)} custom-call(bf16[2,128,2,24,128]{4,3,2,1,0:T(8,128)(2,1)} %velocity.3, bf16[384,384]{1,0:T(8,128)(2,1)} %constant.64.clone.along_x, bf16[128,128]{1,0:T(8,128)(2,1)} %constant.65.clone.along_z, bf16[384,384]{1,0:T(8,128)(2,1)} %constant.62.clone.order), custom_call_target="tpu_custom_call" | custom-call | tf_op jit(solution)/shard_map/inner/pallas_call | solution.py:251
  36.4 0.0 collective-permute-done.2.left_u
  36.4 0.0 collective-permute-done.3.right_u
  36.4 0.0 collective-permute-done.left_w
  36.5 0.0 collective-permute-done.1.right_w
  36.5 0.6 copy-done.2
  37.1 0.1 copy-done.3
  37.1 0.1 copy-done
  37.2 0.7 copy-done.1
  37.9 4.8 %gram.1 = (bf16[48,128,128]{2,1,0:T(8,128)(2,1)}, f32[64,384]{1,0:T(8,128)}) custom-call(f32[48,128,128]{2,1,0:T(8,128)} %inner.1, bf16[3,2,128,128]{3,2,1,0:T(8,128)(2,1)} %copy-done, bf16[3,2,128,128]{3,2,1,0:T(8,128)(2,1)} %copy-done.1, bf16[128,384]{1,0:T(8,128)(2,1)} %copy-done.2, bf16[128,384]{1,0:T(8,128)(2,1)} %copy-done.3, ...), custom_call_target="tpu_custom_call" | custom-call | tf_op jit(solution)/shard_map/gram/pallas_call | solution.py:260
  42.7 1.0 copy.17
  43.7 22.0 %all_to_all.23 = f32[64,1,384]{2,1,0:T(1,128)S(1)} all-to-all(f32[64,1,384]{2,1,0:T(1,128)S(1)} %copy.17), channel_id=1, replica_groups=mesh['gx'=64,'gz'=12] {'gx'}, dimensions={0} | all-to-all | bytes 196608 | tf_op jit(solution)/shard_map/all_to_all | solution.py:210
  65.6 0.1 reduce_sum.18
  65.8 13.0 %all_to_all.24 = f32[12,1,384]{2,1,0:T(1,128)S(1)} all-to-all(f32[12,1,384]{2,1,0:T(1,128)S(1)} %tile.4), channel_id=1, replica_groups=mesh['gx'=64,'gz'=12] {'gz'}, dimensions={0} | all-to-all | bytes 36864 | tf_op jit(solution)/shard_map/all_to_all | solution.py:210
  78.8 0.1 tile.5
  78.9 15.8 %all_to_all.25 = f32[64,1,384]{2,1,0:T(1,128)S(1)} all-to-all(f32[64,1,384]{2,1,0:T(1,128)S(1)} %tile.5), channel_id=1, replica_groups=mesh['gx'=64,'gz'=12] {'gx'}, dimensions={0} | all-to-all | bytes 196608 | tf_op jit(solution)/shard_map/all_to_all | solution.py:210
  94.7 0.6 copy.20
  95.4 11.2 %modes.1 = (bf16[64,2,24,128]{3,2,1,0:T(8,128)(2,1)}, f32[64,128]{1,0:T(8,128)}) custom-call(f32[64,384]{1,0:T(8,128)} %bitcast.9, s32[1,128]{1,0:T(1,128)} %bitcast.12, f32[64,128]{1,0:T(8,128)} %bitcast.11, bf16[48,128,128]{2,1,0:T(8,128)(2,1)} %get-tuple-element.15.vort), custom_call_target="tpu_custom_call" | custom-call | tf_op jit(solution)/shard_map/modes/pallas_call | solution.py:272
  (9 shorter events, 0.1 us)
Async XLA Ops:
  0.6 28.8 %copy-start.4 = (s32[64]{0:T(128)S(1)}, s32[64]{0:T(128)}, u32[]{:S(2)}) copy-start(s32[64]{0:T(128)} %param.13) | copy-start | bytes 772
  6.5 29.9 %collective-permute-start.2 = (bf16[128,384]{1,0:T(8,128)(2,1)}, bf16[128,384]{1,0:T(8,128)(2,1)S(1)}, u32[]{:S(2)}, u32[]{:S(2)}) collective-permute-start(bf16[128,384]{1,0:T(8,128)(2,1)} %get-tuple-element.12), channel_id=1, source_target_pairs={{0,1},{1,2},{2,3},{3,4},{4,5},{5,6},{6,7},{7,8},{8,9},{9,10},{10,1... | collective-permute-start | bytes 294920 | tf_op jit(solution)/shard_map/ppermute | solution.py:206
  11.3 25.1 %collective-permute-start.3 = (bf16[128,384]{1,0:T(8,128)(2,1)}, bf16[128,384]{1,0:T(8,128)(2,1)S(1)}, u32[]{:S(2)}, u32[]{:S(2)}) collective-permute-start(bf16[128,384]{1,0:T(8,128)(2,1)} %get-tuple-element.13), channel_id=1, source_target_pairs={{0,11},{1,0},{2,1},{3,2},{4,3},{5,4},{6,5},{7,6},{8,7},{9,8},{10,9... | collective-permute-start | bytes 294920 | tf_op jit(solution)/shard_map/ppermute | solution.py:206
  23.6 12.9 %collective-permute-start = (bf16[3,2,128,128]{3,2,1,0:T(8,128)(2,1)}, bf16[3,2,128,128]{3,2,1,0:T(8,128)(2,1)S(1)}, u32[]{:S(2)}, u32[]{:S(2)}) collective-permute-start(bf16[3,2,128,128]{3,2,1,0:T(8,128)(2,1)} %get-tuple-element.10), channel_id=1, source_target_pairs={{0,12},{12,24},{24,36},{36,48},{48,60},{60,72},{72,84},{84,96},{96... | collective-permute-start | bytes 589832 | tf_op jit(solution)/shard_map/ppermute | solution.py:206
  27.5 8.9 %collective-permute-start.1 = (bf16[3,2,128,128]{3,2,1,0:T(8,128)(2,1)}, bf16[3,2,128,128]{3,2,1,0:T(8,128)(2,1)S(1)}, u32[]{:S(2)}, u32[]{:S(2)}) collective-permute-start(bf16[3,2,128,128]{3,2,1,0:T(8,128)(2,1)} %get-tuple-element.11), channel_id=1, source_target_pairs={{0,756},{12,0},{24,12},{36,24},{48,36},{60,48},{72,60},{84,72},{96... | collective-permute-start | bytes 589832 | tf_op jit(solution)/shard_map/ppermute | solution.py:206
  36.4 0.6 copy-start.2
  36.4 0.7 copy-start.3
  36.4 0.7 copy-start
  37.2 0.7 copy-start.1

commit v3 on v2

v3 whole, which is shorter than its diff:
```python
from functools import partial

import jax
import jax.numpy as jnp
from jax import lax
from jax.experimental import pallas as pl
from jax.experimental.pallas import tpu as pltpu
from jax.sharding import PartitionSpec as P

ITERS = 3
REACH = 3
TAPS = (45.0, -9.0, 1.0)
TAP_SUM = 60.0
GROUP = 8
FEW = 4
KERNEL_VMEM = 16 << 20
HIGHEST = lax.Precision.HIGHEST
NT = (((1,), (1,)), ((), ()))
TN = (((0,), (0,)), ((), ()))


def tap(offset):
    size = abs(offset)
    if size < 1 or size > REACH:
        return 0.0
    return TAPS[size - 1] if offset > 0 else -TAPS[size - 1]


def taps_at(offset):
    value = jnp.zeros(offset.shape, jnp.float32)
    for size in range(1, REACH + 1):
        value = jnp.where(offset == size, TAPS[size - 1], value)
        value = jnp.where(offset == -size, -TAPS[size - 1], value)
    return value


def index(shape, axis):
    return lax.broadcasted_iota(jnp.int32, shape, axis)


def twice(table):
    zero = jnp.zeros_like(table)
    return jnp.concatenate(
        [jnp.concatenate([table, zero], axis=1), jnp.concatenate([zero, table], axis=1)], axis=0
    ).astype(jnp.bfloat16)


def along_x_table(blocks, cols_x):
    shape = (blocks * cols_x, blocks * cols_x)
    row, col = index(shape, 0), index(shape, 1)
    inside = lax.div(row, cols_x) == lax.div(col, cols_x)
    return jnp.where(inside, taps_at(col - row), 0.0).astype(jnp.bfloat16)


def along_z_table(cols_z):
    shape = (cols_z, cols_z)
    return twice(-taps_at(index(shape, 0) - index(shape, 1)))


def edge_z_table(cols_z):
    shape = (2 * GROUP, cols_z)
    row, col = index(shape, 0), index(shape, 1)
    ahead = jnp.where(row < REACH, taps_at(cols_z + row - col), 0.0)
    behind = jnp.where((row >= GROUP) & (row < GROUP + REACH), taps_at(row - GROUP - REACH - col), 0.0)
    return twice(-(ahead + behind))


def ends_z_table(cols_z):
    shape = (2 * GROUP, cols_z)
    row, col = index(shape, 0), index(shape, 1)
    ahead = (row < REACH) & (col == row)
    behind = (row >= GROUP) & (row < GROUP + REACH) & (col == cols_z - REACH + row - GROUP)
    return jnp.where(ahead | behind, 1.0, 0.0).astype(jnp.bfloat16)


def matmul(left, right, dims=None):
    dims = dims or (((1,), (0,)), ((), ()))
    return lax.dot_general(left, right, dims, preferred_element_type=jnp.float32)


def flat_rows(velocity, field, start, count):
    block = velocity[field, start : start + count]
    return block.reshape(-1, block.shape[-1])


def two_blocks(velocity, field, start):
    blocks = [flat_rows(velocity, field, start + at, FEW) for at in (0, FEW)]
    return jnp.concatenate(blocks, axis=1)


def sides_kernel(velocity, head, tail, first_rows, last_rows):
    reach, planes, snaps, cols_z = head.shape
    cols_x = velocity.shape[3]
    first_rows[...] = velocity[1, :, :, :GROUP].reshape(first_rows.shape).astype(jnp.float32)
    last_rows[...] = velocity[1, :, :, cols_x - GROUP :].reshape(last_rows.shape).astype(jnp.float32)
    stride = planes * GROUP
    for p in range(planes):
        for h in range(reach):
            at = p * GROUP + h
            head[h, p] = first_rows[pl.ds(at, snaps, stride=stride), :].astype(jnp.bfloat16)
            at = (p + 1) * GROUP - reach + h
            tail[h, p] = last_rows[pl.ds(at, snaps, stride=stride), :].astype(jnp.bfloat16)


def span_kernel(velocity, passed, head, tail, passed_on):
    snaps, planes, cols_x = velocity.shape[1:4]
    share = 2 * GROUP
    ends_z = ends_z_table(velocity.shape[4])
    passed_on[...] = passed[...]
    for start in range(0, snaps, share):
        span = slice(start * planes * cols_x, (start + share) * planes * cols_x)
        cols = matmul(ends_z, flat_rows(velocity, 0, start, share), NT).astype(jnp.bfloat16)
        head[:, span] = cols[:GROUP]
        tail[:, span] = cols[GROUP:]


def inner_kernel(velocity, out):
    planes, cols_x, cols_z = velocity.shape[2:]
    count = FEW * planes * cols_x
    along_x = along_x_table(FEW * planes, cols_x)
    along_z = along_z_table(cols_z)
    for q in range(velocity.shape[1] // (2 * FEW)):
        value = matmul(along_x, two_blocks(velocity, 1, 2 * FEW * q))
        value = value + matmul(two_blocks(velocity, 0, 2 * FEW * q), along_z)
        for half in range(2):
            at = (2 * q + half) * count
            out[at : at + count, :] = value[:, half * cols_z : (half + 1) * cols_z]


def gram_kernel(inner, left_w, right_w, left_u, right_u, place, vort, rows_out, work):
    lines, snaps, cols_z = vort.shape
    planes = left_w.shape[1]
    cols_x = lines // planes
    kept = place.shape[1]
    count = lines * GROUP
    edge_z = edge_z_table(cols_z)
    for q in range(snaps // (2 * GROUP)):
        spans = [slice((2 * q + half) * count, (2 * q + half + 1) * count) for half in range(2)]
        cols = jnp.concatenate([side[:, span] for span in spans for side in (right_u, left_u)], axis=0)
        value = matmul(cols, edge_z, TN)
        for half in range(2):
            work[spans[half], :] = inner[spans[half], :] + value[:, half * cols_z : (half + 1) * cols_z]
    gram = jnp.zeros((snaps + kept, snaps), jnp.float32)
    lane = lax.broadcasted_iota(jnp.int32, (kept, 2 * cols_z), 1).astype(jnp.float32)
    down = jnp.broadcast_to(place[...].astype(jnp.float32), (GROUP, kept)).T[:, :1]
    for pair in range(lines // 2):
        sides = []
        for line in (2 * pair, 2 * pair + 1):
            p, x = line // cols_x, line % cols_x
            value = work[pl.ds(line, snaps, stride=lines), :]
            for h in range(REACH):
                if tap(cols_x + h - x):
                    value = value + tap(cols_x + h - x) * right_w[h, p].astype(jnp.float32)
                if tap(h - REACH - x):
                    value = value + tap(h - REACH - x) * left_w[h, p].astype(jnp.float32)
            value = (value * (1.0 / TAP_SUM)).astype(jnp.bfloat16)
            vort[line] = value
            sides.append(value)
        both = jnp.concatenate(sides, axis=1)
        chosen = jnp.where(lane == down - float(2 * pair * cols_z), 1.0, 0.0).astype(jnp.bfloat16)
        gram = gram + matmul(jnp.concatenate([both, chosen], axis=0), both, NT)
    for part in range((snaps + kept) // kept):
        rows_out[:, 0, part * snaps : (part + 1) * snaps] = gram[part * kept : (part + 1) * kept]


def spread(tile, row):
    return jnp.broadcast_to(tile[row : row + 1], tile.shape)


def orthonormal_rows(block, inner):
    kept, snaps = block.shape
    shape = (GROUP, snaps)
    count = kept // GROUP
    row_at = index(shape, 0)
    inner = jnp.concatenate([inner, jnp.zeros((kept, snaps - kept), inner.dtype)], axis=1)
    inner_rows = [inner[GROUP * i : GROUP * (i + 1)] for i in range(count)]
    block_rows = [block[GROUP * i : GROUP * (i + 1)] for i in range(count)]
    for b in range(count):
        cols = []
        for t in range(GROUP):
            at = GROUP * b + t
            cols.append([jnp.broadcast_to(rows[:, at : at + 1], shape) for rows in inner_rows[b:]])
        pivot = [[spread(cols[t][0], i) for i in range(GROUP)] for t in range(GROUP)]
        cols = [col[1:] for col in cols]
        inner_at = [spread(inner_rows[b], t) for t in range(GROUP)]
        block_at = [spread(block_rows[b], t) for t in range(GROUP)]
        done = jnp.zeros(shape, jnp.float32)
        for t in range(GROUP):
            root = lax.rsqrt(pivot[t][t])
            inverse = root * root
            for later in range(t + 1, GROUP):
                part = pivot[t][later] * inverse
                for i in range(later, GROUP):
                    pivot[later][i] = pivot[later][i] - pivot[t][i] * part
                inner_at[later] = inner_at[later] - inner_at[t] * part
                block_at[later] = block_at[later] - block_at[t] * part
                cols[later] = [col - first * part for col, first in zip(cols[later], cols[t])]
            done = jnp.where(row_at == t, block_at[t] * root, done)
            inner_part = inner_at[t] * inverse
            block_part = block_at[t] * inverse
            for r in range(b + 1, count):
                inner_rows[r] = inner_rows[r] - cols[t][r - b - 1] * inner_part
                block_rows[r] = block_rows[r] - cols[t][r - b - 1] * block_part
        block_rows[b] = done
    return jnp.concatenate(block_rows, axis=0)


def modes_kernel(cells, rows, rank, start, vort, modes, basis, work):
    kept, snaps = start.shape
    lines = vort.shape[0]
    parts = [rows[:, 0, b * snaps : (b + 1) * snaps] for b in range(snaps // kept + 1)]
    gram = jnp.concatenate(parts[:-1], axis=0) * (1.0 / cells)
    picked = parts[-1]
    scale = jnp.where(rank[...] < kept, 1.0, 0.25).astype(jnp.float32)
    now = start[...]
    for step in range(ITERS):
        block = lax.dot_general(now * scale, gram, NT, precision=HIGHEST, preferred_element_type=jnp.float32)
        block = block * scale
        inner = lax.dot_general(block, block, NT, precision=HIGHEST, preferred_element_type=jnp.float32)
        now = orthonormal_rows(block, inner)
    coef = (now * scale).astype(jnp.bfloat16)
    anchor = jnp.sum(picked * coef.astype(jnp.float32), axis=1, keepdims=True)
    orient = anchor / jnp.maximum(jnp.abs(anchor), 1.0)
    basis[...] = now * orient
    for line in range(lines):
        work[pl.ds(line, kept, stride=lines), :] = matmul(coef, vort[line]) * orient
    modes[...] = work[...].astype(jnp.bfloat16).reshape(modes.shape)


def local_place(anchor_index, planes, cols_x, cols_z, total_x, total_z):
    plane_of = anchor_index // (total_x * total_z)
    remain = anchor_index % (total_x * total_z)
    local_x = remain // total_z - lax.axis_index("gx") * cols_x
    local_z = remain % total_z - lax.axis_index("gz") * cols_z
    owned = (local_x >= 0) & (local_x < cols_x) & (local_z >= 0) & (local_z < cols_z)
    return jnp.where(owned, (plane_of * cols_x + local_x) * cols_z + local_z, -1)


def shifted(value, axis, step):
    count = lax.axis_size(axis)
    return lax.ppermute(value, axis, [(i, (i + step) % count) for i in range(count)])


def exchanged(rows, axis):
    return lax.all_to_all(rows, axis, 0, 0, tiled=True)


def summed(rows, axis):
    count = lax.axis_size(axis)
    return jnp.sum(rows.reshape((count, rows.shape[0] // count) + rows.shape[1:]), axis=0)


def copies(rows, axis):
    return jnp.tile(rows, (lax.axis_size(axis),) + (1,) * (rows.ndim - 1))


def near(shape, dtype):
    return pltpu.VMEM(shape, dtype)


def local_call(kernel, outs, name, scratch=()):
    def run(*args):
        return pl.pallas_call(
            kernel,
            in_specs=[pl.BlockSpec(memory_space=pltpu.VMEM)] * len(args),
            out_specs=[pl.BlockSpec(memory_space=pltpu.VMEM)] * len(outs),
            out_shape=outs,
            scratch_shapes=list(scratch),
            compiler_params=pltpu.CompilerParams(vmem_limit_bytes=KERNEL_VMEM),
            name=name,
        )(*[pltpu.with_memory_space_constraint(arg, pltpu.VMEM) for arg in args])

    return run


def body(velocity, snapshot_rank, anchor_index, start_basis):
    _, snaps, planes, cols_x, cols_z = velocity.shape
    kept = start_basis.shape[1]
    lines = planes * cols_x
    total_x = cols_x * lax.axis_size("gx")
    total_z = cols_z * lax.axis_size("gz")
    side = near((REACH, planes, snaps, cols_z), jnp.bfloat16)
    strip = near((GROUP, snaps * lines), jnp.bfloat16)
    rows_at = pltpu.VMEM((snaps * planes * GROUP, cols_z), jnp.float32)
    head_w, tail_w = local_call(sides_kernel, [side, side], "sides", [rows_at] * 2)(velocity)
    left_w = shifted(tail_w, "gx", 1)
    head_u, tail_u, head_w = local_call(span_kernel, [strip, strip, side], "span")(velocity, head_w)
    right_w = shifted(head_w, "gx", -1)
    left_u = shifted(tail_u, "gz", 1)
    right_u = shifted(head_u, "gz", -1)
    field = near((snaps * lines, cols_z), jnp.float32)
    (inner,) = local_call(inner_kernel, [field], "inner")(velocity)
    place = local_place(anchor_index, planes, cols_x, cols_z, total_x, total_z)
    vort, rows = local_call(
        gram_kernel,
        [
            near((lines, snaps, cols_z), jnp.bfloat16),
            near((kept, 1, (snaps // kept + 1) * snaps), jnp.float32),
        ],
        "gram",
        [field],
    )(inner, left_w, right_w, left_u, right_u, place[None, :])
    mine = summed(exchanged(rows, "gx"), "gx")
    mine = summed(exchanged(copies(mine, "gz"), "gz"), "gz")
    rows = exchanged(copies(mine, "gx"), "gx")
    modes, basis = local_call(
        partial(modes_kernel, float(planes * total_x * total_z)),
        [
            jax.ShapeDtypeStruct((kept, planes, cols_x, cols_z), jnp.bfloat16),
            jax.ShapeDtypeStruct((kept, snaps), jnp.float32),
        ],
        "modes",
        [pltpu.VMEM((kept * lines, cols_z), jnp.float32)],
    )(rows, snapshot_rank[None, :], start_basis.T, vort)
    return modes, basis.T


def solution(mesh):
    return jax.shard_map(
        body,
        mesh=mesh,
        in_specs=(P(None, None, None, "gx", "gz"), P(), P(), P()),
        out_specs=(P(None, None, "gx", "gz"), P()),
        check_vma=False,
    )
```

time: 107 us -> 96.7 us (0.904)
  Pallas kernels: 28.1 us -> 15.4 us
  waiting for transfers between devices: 0.01 us -> 4.15 us
  local copies, waits for them, and re-layouts: 3.83 us -> 1.97 us
    pallas_call x4 -> x5, Pallas kernels: 28.1 us -> 15.4 us  [run(): pl.pallas_call(kernel, in_specs=[pl.BlockSpec(memory_space=pltpu.VMEM)] *...]
    ppermute x4, waiting for transfers between devices: 0.01 us -> 4.15 us  [shifted(): lax.ppermute(value, axis, [(i, (i + step) % count) for i in range(count)])]
  transfers between devices with their start and end apart: 4 -> 4, of which waited for: 0 -> 1; matrix products, arithmetic and copies ran while one was open for 1% -> 0% of each run, Pallas kernels for 6% -> 2%
where the time goes in v3:
time: 96.7 us; the launch traced here: 96.3 us
  blocking collectives  51.2 us (53%)
  starting transfers between devices  22.6 us (23%)
  Pallas kernels  15.4 us (16%)
  waiting for transfers between devices  4.15 us (4%)
  local copies, waits for them, and re-layouts  1.97 us (2%)
    all_to_all x3, blocking collectives, exchanged(): return lax.all_to_all(rows, axis, 0, 0, tiled=True)  51.2 us
    ppermute x4, starting transfers between devices, shifted(): lax.ppermute(value, axis, [(i, (i + step) % count) for i in range(count)])  22.6 us
    pallas_call x5, Pallas kernels, run(): pl.pallas_call(kernel, in_specs=[pl.BlockSpec(memory_space=pltpu.VMEM)] *...  15.4 us
    ppermute x4, waiting for transfers between devices, shifted(): lax.ppermute(value, axis, [(i, (i + step) % count) for i in range(count)])  4.15 us
  transfers between devices with their start and end apart: 4, of which 1 were waited for; matrix products, arithmetic and copies ran while one was open for 0% of the time, Pallas kernels for 2%

profile of v3, /device:TPU:1, one launch (start us, length us, event | category | flops | bytes accessed | tf_op | source)
XLA Modules:
  0.0 96.3 jit_solution(6761547005572787239)
XLA Ops:
  0.6 0.0 copy-start
  0.6 1.9 %copy-done = bf16[2,128,2,24,128]{4,3,2,1,0:T(8,128)(2,1)S(1)} copy-done((bf16[2,128,2,24,128]{4,3,2,1,0:T(8,128)(2,1)S(1)}, bf16[2,128,2,24,128]{4,3,2,1,0:T(8,128)(2,1)}, u32[]{:S(2)}) %copy-start) | copy-done | bytes 3145752
  2.5 1.0 %sides.1 = (bf16[3,2,128,128]{3,2,1,0:T(8,128)(2,1)S(1)}, bf16[3,2,128,128]{3,2,1,0:T(8,128)(2,1)}) custom-call(bf16[2,128,2,24,128]{4,3,2,1,0:T(8,128)(2,1)S(1)} %copy-done), custom_call_target="tpu_custom_call" | custom-call | tf_op jit(solution)/shard_map/sides/pallas_call | solution.py:263
  3.6 4.5 %collective-permute-start = (bf16[3,2,128,128]{3,2,1,0:T(8,128)(2,1)}, bf16[3,2,128,128]{3,2,1,0:T(8,128)(2,1)S(1)}, u32[]{:S(2)}, u32[]{:S(2)}) collective-permute-start(bf16[3,2,128,128]{3,2,1,0:T(8,128)(2,1)} %get-tuple-element.11), channel_id=1, source_target_pairs={{0,12},{12,24},{24,36},{36,48},{48,60},{60,72},{72,84},{84,96},{96... | collective-permute-start | bytes 589832 | tf_op jit(solution)/shard_map/ppermute | solution.py:241
  8.1 1.3 %span.1 = (bf16[8,6144]{1,0:T(8,128)(2,1)}, bf16[8,6144]{1,0:T(8,128)(2,1)}, bf16[3,2,128,128]{3,2,1,0:T(8,128)(2,1)}) custom-call(bf16[2,128,2,24,128]{4,3,2,1,0:T(8,128)(2,1)S(1)} %copy-done, bf16[3,2,128,128]{3,2,1,0:T(8,128)(2,1)S(1)} %get-tuple-element.12.passed), custom_call_target="tpu_custom_call" | custom-call | tf_op jit(solution)/shard_map/span/pallas_call | solution.py:263
  9.3 4.0 %collective-permute-start.2 = (bf16[8,6144]{1,0:T(8,128)(2,1)}, bf16[8,6144]{1,0:T(8,128)(2,1)}, u32[]{:S(2)}, u32[]{:S(2)}) collective-permute-start(bf16[8,6144]{1,0:T(8,128)(2,1)} %get-tuple-element.14), channel_id=1, source_target_pairs={{0,1},{1,2},{2,3},{3,4},{4,5},{5,6},{6,7},{7,8},{8,9},{9,10},{10,1... | collective-permute-start | bytes 294920 | tf_op jit(solution)/shard_map/ppermute | solution.py:241
  13.3 12.2 %collective-permute-start.3 = (bf16[8,6144]{1,0:T(8,128)(2,1)}, bf16[8,6144]{1,0:T(8,128)(2,1)}, u32[]{:S(2)}, u32[]{:S(2)}) collective-permute-start(bf16[8,6144]{1,0:T(8,128)(2,1)} %get-tuple-element.15), channel_id=1, source_target_pairs={{0,11},{1,0},{2,1},{3,2},{4,3},{5,4},{6,5},{7,6},{8,7},{9,8},{10,9... | collective-permute-start | bytes 294920 | tf_op jit(solution)/shard_map/ppermute | solution.py:241
  25.6 1.9 %collective-permute-start.1 = (bf16[3,2,128,128]{3,2,1,0:T(8,128)(2,1)}, bf16[3,2,128,128]{3,2,1,0:T(8,128)(2,1)S(1)}, u32[]{:S(2)}, u32[]{:S(2)}) collective-permute-start(bf16[3,2,128,128]{3,2,1,0:T(8,128)(2,1)} %get-tuple-element.13), channel_id=1, source_target_pairs={{0,756},{12,0},{24,12},{36,24},{48,36},{60,48},{72,60},{84,72},{96... | collective-permute-start | bytes 589832 | tf_op jit(solution)/shard_map/ppermute | solution.py:241
  27.5 0.0 copy-done.4
  27.6 0.0 copy-done.1
  27.6 1.0 %inner.1 = f32[6144,128]{1,0:T(8,128)S(1)} custom-call(bf16[2,128,2,24,128]{4,3,2,1,0:T(8,128)(2,1)S(1)} %copy-done.1), custom_call_target="tpu_custom_call" | custom-call | tf_op jit(solution)/shard_map/inner/pallas_call | solution.py:263
  28.6 0.0 copy-start.2
  28.6 0.0 copy-start.3
  28.6 0.0 collective-permute-done.2.left_u
  28.6 0.0 collective-permute-done.3.right_u
  28.6 0.0 collective-permute-done.left_w
  28.6 4.1 %collective-permute-done.1.right_w = bf16[3,2,128,128]{3,2,1,0:T(8,128)(2,1)S(1)} collective-permute-done((bf16[3,2,128,128]{3,2,1,0:T(8,128)(2,1)}, bf16[3,2,128,128]{3,2,1,0:T(8,128)(2,1)S(1)}, u32[]{:S(2)}, u32[]{:S(2)}) %collective-permute-start.1) | collective-permute-done | bytes 196640 | tf_op jit(solution)/shard_map/ppermute | solution.py:241
  32.8 3.3 %gram.1 = (bf16[48,128,128]{2,1,0:T(8,128)(2,1)S(1)}, f32[64,1,384]{2,1,0:T(1,128)S(1)}) custom-call(f32[6144,128]{1,0:T(8,128)S(1)} %inner.1, bf16[3,2,128,128]{3,2,1,0:T(8,128)(2,1)S(1)} %collective-permute-done.left_w, bf16[3,2,128,128]{3,2,1,0:T(8,128)(2,1)S(1)} %collective-permute-done.1.right_w, bf16[8,6144]{1,0:T(8,128)(2,1)} %collective-permute-done.2.left_u, ...), custom_call_target="tpu_custom_call" | custom-call | tf_op jit(solution)/shard_map/gram/pallas_call | solution.py:263
  36.1 22.6 %all_to_all.15 = f32[64,1,384]{2,1,0:T(1,128)S(1)} all-to-all(f32[64,1,384]{2,1,0:T(1,128)S(1)} %get-tuple-element.16), channel_id=1, replica_groups=mesh['gx'=64,'gz'=12] {'gx'}, dimensions={0} | all-to-all | bytes 196608 | tf_op jit(solution)/shard_map/all_to_all | solution.py:245
  58.7 0.1 reduce_sum.18
  58.8 12.8 %all_to_all.16 = f32[12,1,384]{2,1,0:T(1,128)S(1)} all-to-all(f32[12,1,384]{2,1,0:T(1,128)S(1)} %tile.4), channel_id=1, replica_groups=mesh['gx'=64,'gz'=12] {'gz'}, dimensions={0} | all-to-all | bytes 36864 | tf_op jit(solution)/shard_map/all_to_all | solution.py:245
  71.6 0.1 tile.5
  71.6 15.8 %all_to_all.17.rows = f32[64,1,384]{2,1,0:T(1,128)S(1)} all-to-all(f32[64,1,384]{2,1,0:T(1,128)S(1)} %tile.5), channel_id=1, replica_groups=mesh['gx'=64,'gz'=12] {'gx'}, dimensions={0} | all-to-all | bytes 196608 | tf_op jit(solution)/shard_map/all_to_all | solution.py:245
  87.5 8.8 %modes.1 = (bf16[64,2,24,128]{3,2,1,0:T(8,128)(2,1)}, f32[64,128]{1,0:T(8,128)}) custom-call(f32[64,1,384]{2,1,0:T(1,128)S(1)} %all_to_all.17.rows, s32[1,128]{1,0:T(1,128)S(1)} %bitcast.6, f32[64,128]{1,0:T(8,128)S(1)} %bitcast.5, bf16[48,128,128]{2,1,0:T(8,128)(2,1)S(1)} %get-tuple-element.17.vort), custom_call_target="tpu_custom_call" | custom-call | tf_op jit(solution)/shard_map/modes/pallas_call | solution.py:263
  (7 shorter events, 0.1 us)
Async XLA Ops:
  0.6 1.9 %copy-start = (bf16[2,128,2,24,128]{4,3,2,1,0:T(8,128)(2,1)S(1)}, bf16[2,128,2,24,128]{4,3,2,1,0:T(8,128)(2,1)}, u32[]{:S(2)}) copy-start(bf16[2,128,2,24,128]{4,3,2,1,0:T(8,128)(2,1)} %velocity.5) | copy-start | bytes 9437188
  2.5 25.0 %copy-start.4 = (s32[64]{0:T(128)S(1)}, s32[64]{0:T(128)}, u32[]{:S(2)}) copy-start(s32[64]{0:T(128)} %param.6) | copy-start | bytes 772
  2.5 25.0 %copy-start.1 = (bf16[2,128,2,24,128]{4,3,2,1,0:T(8,128)(2,1)S(1)}, bf16[2,128,2,24,128]{4,3,2,1,0:T(8,128)(2,1)}, u32[]{:S(2)}) copy-start(bf16[2,128,2,24,128]{4,3,2,1,0:T(8,128)(2,1)} %velocity.5) | copy-start | bytes 9437188
  3.6 25.1 %collective-permute-start = (bf16[3,2,128,128]{3,2,1,0:T(8,128)(2,1)}, bf16[3,2,128,128]{3,2,1,0:T(8,128)(2,1)S(1)}, u32[]{:S(2)}, u32[]{:S(2)}) collective-permute-start(bf16[3,2,128,128]{3,2,1,0:T(8,128)(2,1)} %get-tuple-element.11), channel_id=1, source_target_pairs={{0,12},{12,24},{24,36},{36,48},{48,60},{60,72},{72,84},{84,96},{96... | collective-permute-start | bytes 589832 | tf_op jit(solution)/shard_map/ppermute | solution.py:241
  9.3 19.3 %collective-permute-start.2 = (bf16[8,6144]{1,0:T(8,128)(2,1)}, bf16[8,6144]{1,0:T(8,128)(2,1)}, u32[]{:S(2)}, u32[]{:S(2)}) collective-permute-start(bf16[8,6144]{1,0:T(8,128)(2,1)} %get-tuple-element.14), channel_id=1, source_target_pairs={{0,1},{1,2},{2,3},{3,4},{4,5},{5,6},{6,7},{7,8},{8,9},{9,10},{10,1... | collective-permute-start | bytes 294920 | tf_op jit(solution)/shard_map/ppermute | solution.py:241
  13.3 15.3 %collective-permute-start.3 = (bf16[8,6144]{1,0:T(8,128)(2,1)}, bf16[8,6144]{1,0:T(8,128)(2,1)}, u32[]{:S(2)}, u32[]{:S(2)}) collective-permute-start(bf16[8,6144]{1,0:T(8,128)(2,1)} %get-tuple-element.15), channel_id=1, source_target_pairs={{0,11},{1,0},{2,1},{3,2},{4,3},{5,4},{6,5},{7,6},{8,7},{9,8},{10,9... | collective-permute-start | bytes 294920 | tf_op jit(solution)/shard_map/ppermute | solution.py:241
  25.6 7.2 %collective-permute-start.1 = (bf16[3,2,128,128]{3,2,1,0:T(8,128)(2,1)}, bf16[3,2,128,128]{3,2,1,0:T(8,128)(2,1)S(1)}, u32[]{:S(2)}, u32[]{:S(2)}) collective-permute-start(bf16[3,2,128,128]{3,2,1,0:T(8,128)(2,1)} %get-tuple-element.13), channel_id=1, source_target_pairs={{0,756},{12,0},{24,12},{36,24},{48,36},{60,48},{72,60},{84,72},{96... | collective-permute-start | bytes 589832 | tf_op jit(solution)/shard_map/ppermute | solution.py:241
  28.6 58.9 %copy-start.2 = (f32[128,64]{0,1:T(8,128)S(1)}, f32[128,64]{0,1:T(8,128)}, u32[]{:S(2)}) copy-start(f32[128,64]{0,1:T(8,128)} %param.7) | copy-start | bytes 98308
  28.6 58.9 %copy-start.3 = (s32[128]{0:T(128)S(1)}, s32[128]{0:T(128)}, u32[]{:S(2)}) copy-start(s32[128]{0:T(128)} %param.5) | copy-start | bytes 1540

commit v4 on v3

--- a/solution.py
+++ b/solution.py
@@ -1,3 +1,4 @@
+import math
 from functools import partial
 
 import jax
@@ -8,11 +9,16 @@
 from jax.sharding import PartitionSpec as P
 
 ITERS = 3
+CHIPS = "chips"
+CORES = "cores"
+GX = (CHIPS, CORES)
+GZ = "gz"
 REACH = 3
 TAPS = (45.0, -9.0, 1.0)
 TAP_SUM = 60.0
 GROUP = 8
 FEW = 4
+PIECES = 16
 KERNEL_VMEM = 16 << 20
 HIGHEST = lax.Precision.HIGHEST
 NT = (((1,), (1,)), ((), ()))
@@ -88,18 +94,25 @@
     return jnp.concatenate(blocks, axis=1)
 
 
-def sides_kernel(velocity, head, tail, first_rows, last_rows):
+def sides_kernel(velocity, head, tail, first, last, first_rows, last_rows, landed):
     reach, planes, snaps, cols_z = head.shape
     cols_x = velocity.shape[3]
-    first_rows[...] = velocity[1, :, :, :GROUP].reshape(first_rows.shape).astype(jnp.float32)
-    last_rows[...] = velocity[1, :, :, cols_x - GROUP :].reshape(last_rows.shape).astype(jnp.float32)
+    first_copy = pltpu.make_async_copy(velocity.at[1, :, :, pl.ds(0, GROUP)], first, landed.at[0])
+    last_copy = pltpu.make_async_copy(velocity.at[1, :, :, pl.ds(cols_x - GROUP, GROUP)], last, landed.at[1])
+    first_copy.start()
+    last_copy.start()
     stride = planes * GROUP
-    for p in range(planes):
-        for h in range(reach):
-            at = p * GROUP + h
-            head[h, p] = first_rows[pl.ds(at, snaps, stride=stride), :].astype(jnp.bfloat16)
-            at = (p + 1) * GROUP - reach + h
-            tail[h, p] = last_rows[pl.ds(at, snaps, stride=stride), :].astype(jnp.bfloat16)
+    last_start = GROUP - reach
+    for copy, tiles, rows, side, start in (
+        (first_copy, first, first_rows, head, 0),
+        (last_copy, last, last_rows, tail, last_start),
+    ):
+        copy.wait()
+        rows[...] = tiles[...].reshape(rows.shape).astype(jnp.float32)
+        for p in range(planes):
+            for h in range(reach):
+                at = p * GROUP + start + h
+                side[h, p] = rows[pl.ds(at, snaps, stride=stride), :].astype(jnp.bfloat16)
 
 
 def span_kernel(velocity, passed, head, tail, passed_on):
@@ -127,19 +140,23 @@
             out[at : at + count, :] = value[:, half * cols_z : (half + 1) * cols_z]
 
 
-def gram_kernel(inner, left_w, right_w, left_u, right_u, place, vort, rows_out, work):
+def across_kernel(inner, left_u, right_u, out):
+    cols_z = inner.shape[1]
+    count = inner.shape[0] // PIECES
+    edge_z = edge_z_table(cols_z)
+    for q in range(PIECES // 2):
+        spans = [slice((2 * q + half) * count, (2 * q + half + 1) * count) for half in range(2)]
+        cols = jnp.concatenate([side[:, span] for span in spans for side in (right_u, left_u)], axis=0)
+        value = matmul(cols, edge_z, TN)
+        for half in range(2):
+            out[spans[half], :] = inner[spans[half], :] + value[:, half * cols_z : (half + 1) * cols_z]
+
+
+def gram_kernel(inner, left_w, right_w, place, vort, rows_out):
     lines, snaps, cols_z = vort.shape
     planes = left_w.shape[1]
     cols_x = lines // planes
     kept = place.shape[1]
-    count = lines * GROUP
-    edge_z = edge_z_table(cols_z)
-    for q in range(snaps // (2 * GROUP)):
-        spans = [slice((2 * q + half) * count, (2 * q + half + 1) * count) for half in range(2)]
-        cols = jnp.concatenate([side[:, span] for span in spans for side in (right_u, left_u)], axis=0)
-        value = matmul(cols, edge_z, TN)
-        for half in range(2):
-            work[spans[half], :] = inner[spans[half], :] + value[:, half * cols_z : (half + 1) * cols_z]
     gram = jnp.zeros((snaps + kept, snaps), jnp.float32)
     lane = lax.broadcasted_iota(jnp.int32, (kept, 2 * cols_z), 1).astype(jnp.float32)
     down = jnp.broadcast_to(place[...].astype(jnp.float32), (GROUP, kept)).T[:, :1]
@@ -147,7 +164,7 @@
         sides = []
         for line in (2 * pair, 2 * pair + 1):
             p, x = line // cols_x, line % cols_x
-            value = work[pl.ds(line, snaps, stride=lines), :]
+            value = inner[pl.ds(line, snaps, stride=lines), :]
             for h in range(REACH):
                 if tap(cols_x + h - x):
                     value = value + tap(cols_x + h - x) * right_w[h, p].astype(jnp.float32)
@@ -230,14 +247,18 @@
 def local_place(anchor_index, planes, cols_x, cols_z, total_x, total_z):
     plane_of = anchor_index // (total_x * total_z)
     remain = anchor_index % (total_x * total_z)
-    local_x = remain // total_z - lax.axis_index("gx") * cols_x
-    local_z = remain % total_z - lax.axis_index("gz") * cols_z
+    local_x = remain // total_z - lax.axis_index(GX) * cols_x
+    local_z = remain % total_z - lax.axis_index(GZ) * cols_z
     owned = (local_x >= 0) & (local_x < cols_x) & (local_z >= 0) & (local_z < cols_z)
     return jnp.where(owned, (plane_of * cols_x + local_x) * cols_z + local_z, -1)
 
 
+def size_of(axes):
+    return math.prod(lax.axis_size(axis) for axis in ((axes,) if isinstance(axes, str) else axes))
+
+
 def shifted(value, axis, step):
-    count = lax.axis_size(axis)
+    count = size_of(axis)
     return lax.ppermute(value, axis, [(i, (i + step) % count) for i in range(count)])
 
 
@@ -246,29 +267,29 @@
 
 
 def summed(rows, axis):
-    count = lax.axis_size(axis)
+    count = size_of(axis)
     return jnp.sum(rows.reshape((count, rows.shape[0] // count) + rows.shape[1:]), axis=0)
 
 
 def copies(rows, axis):
-    return jnp.tile(rows, (lax.axis_size(axis),) + (1,) * (rows.ndim - 1))
+    return jnp.tile(rows, (size_of(axis),) + (1,) * (rows.ndim - 1))
 
 
 def near(shape, dtype):
     return pltpu.VMEM(shape, dtype)
 
 
-def local_call(kernel, outs, name, scratch=()):
+def local_call(kernel, outs, name, scratch=(), space=pltpu.VMEM):
     def run(*args):
         return pl.pallas_call(
             kernel,
-            in_specs=[pl.BlockSpec(memory_space=pltpu.VMEM)] * len(args),
+            in_specs=[pl.BlockSpec(memory_space=space)] * len(args),
             out_specs=[pl.BlockSpec(memory_space=pltpu.VMEM)] * len(outs),
             out_shape=outs,
             scratch_shapes=list(scratch),
             compiler_params=pltpu.CompilerParams(vmem_limit_bytes=KERNEL_VMEM),
             name=name,
-        )(*[pltpu.with_memory_space_constraint(arg, pltpu.VMEM) for arg in args])
+        )(*[pltpu.with_memory_space_constraint(arg, space) for arg in args])
 
     return run
 
@@ -277,19 +298,22 @@
     _, snaps, planes, cols_x, cols_z = velocity.shape
     kept = start_basis.shape[1]
     lines = planes * cols_x
-    total_x = cols_x * lax.axis_size("gx")
-    total_z = cols_z * lax.axis_size("gz")
+    total_x = cols_x * size_of(GX)
+    total_z = cols_z * size_of(GZ)
     side = near((REACH, planes, snaps, cols_z), jnp.bfloat16)
     strip = near((GROUP, snaps * lines), jnp.bfloat16)
     rows_at = pltpu.VMEM((snaps * planes * GROUP, cols_z), jnp.float32)
-    head_w, tail_w = local_call(sides_kernel, [side, side], "sides", [rows_at] * 2)(velocity)
-    left_w = shifted(tail_w, "gx", 1)
+    tiles = pltpu.VMEM((snaps, planes, GROUP, cols_z), jnp.bfloat16)
+    scratch = [tiles, tiles, rows_at, rows_at, pltpu.SemaphoreType.DMA((2,))]
+    head_w, tail_w = local_call(sides_kernel, [side, side], "sides", scratch, pltpu.HBM)(velocity)
+    left_w = shifted(tail_w, GX, 1)
     head_u, tail_u, head_w = local_call(span_kernel, [strip, strip, side], "span")(velocity, head_w)
-    right_w = shifted(head_w, "gx", -1)
-    left_u = shifted(tail_u, "gz", 1)
-    right_u = shifted(head_u, "gz", -1)
+    right_w = shifted(head_w, GX, -1)
+    left_u = shifted(tail_u, GZ, 1)
+    right_u = shifted(head_u, GZ, -1)
     field = near((snaps * lines, cols_z), jnp.float32)
     (inner,) = local_call(inner_kernel, [field], "inner")(velocity)
+    (inner,) = local_call(across_kernel, [field], "across")(inner, left_u, right_u)
     place = local_place(anchor_index, planes, cols_x, cols_z, total_x, total_z)
     vort, rows = local_call(
         gram_kernel,
@@ -298,11 +322,10 @@
             near((kept, 1, (snaps // kept + 1) * snaps), jnp.float32),
         ],
         "gram",
-        [field],
-    )(inner, left_w, right_w, left_u, right_u, place[None, :])
-    mine = summed(exchanged(rows, "gx"), "gx")
-    mine = summed(exchanged(copies(mine, "gz"), "gz"), "gz")
-    rows = exchanged(copies(mine, "gx"), "gx")
+    )(inner, left_w, right_w, place[None, :])
+    mine = summed(exchanged(rows, CHIPS), CHIPS)
+    mine = summed(exchanged(copies(mine, (CORES, GZ)), (CORES, GZ)), (CORES, GZ))
+    rows = exchanged(copies(mine, CHIPS), CHIPS)
     modes, basis = local_call(
         partial(modes_kernel, float(planes * total_x * total_z)),
         [
@@ -316,10 +339,12 @@
 
 
 def solution(mesh):
+    count_x, count_z = mesh.shape["gx"], mesh.shape["gz"]
+    split = jax.sharding.Mesh(mesh.devices.reshape(count_x // 2, 2, count_z), (CHIPS, CORES, GZ))
     return jax.shard_map(
         body,
-        mesh=mesh,
-        in_specs=(P(None, None, None, "gx", "gz"), P(), P(), P()),
-        out_specs=(P(None, None, "gx", "gz"), P()),
+        mesh=split,
+        in_specs=(P(None, None, None, GX, GZ), P(), P(), P()),
+        out_specs=(P(None, None, GX, GZ), P()),
         check_vma=False,
     )

time: 96.7 us -> 92.4 us (0.956)
  blocking collectives: 51.2 us -> 48.2 us
  waiting for transfers between devices: 4.15 us -> 2.18 us
  local copies, waits for them, and re-layouts: 1.97 us -> 0.43 us
  Pallas kernels: 15.4 us -> 16.6 us
    all_to_all x3, blocking collectives: 51.2 us -> 48.2 us  [exchanged(): return lax.all_to_all(rows, axis, 0, 0, tiled=True)]
    ppermute x4, waiting for transfers between devices: 4.15 us -> 2.18 us  [shifted(): lax.ppermute(value, axis, [(i, (i + step) % count) for i in range(count)])]
    unnamed x10 -> x8, local copies, waits for them, and re-layouts: 1.9 us -> 0.02 us
    pallas_call x5 -> x6, Pallas kernels: 15.4 us -> 16.6 us  [run(): pl.pallas_call(kernel, in_specs=[pl.BlockSpec(memory_space=space)] * len(...]
  transfers between devices with their start and end apart: 4 -> 4, of which waited for: 1 -> 1; matrix products, arithmetic and copies ran while one was open for 0% -> 0% of each run, Pallas kernels for 2% -> 3%
where the time goes in v4:
time: 92.4 us; the launch traced here: 91.7 us
  blocking collectives  48.2 us (52%)
  starting transfers between devices  22.9 us (25%)
  Pallas kernels  16.6 us (18%)
  waiting for transfers between devices  2.18 us (2%)
    all_to_all x3, blocking collectives, exchanged(): return lax.all_to_all(rows, axis, 0, 0, tiled=True)  48.2 us
    ppermute x4, starting transfers between devices, shifted(): lax.ppermute(value, axis, [(i, (i + step) % count) for i in range(count)])  22.9 us
    pallas_call x6, Pallas kernels, run(): pl.pallas_call(kernel, in_specs=[pl.BlockSpec(memory_space=space)] * len(...  16.6 us
    ppermute x4, waiting for transfers between devices, shifted(): lax.ppermute(value, axis, [(i, (i + step) % count) for i in range(count)])  2.18 us
  transfers between devices with their start and end apart: 4, of which 1 were waited for; matrix products, arithmetic and copies ran while one was open for 0% of the time, Pallas kernels for 3%

profile of v4, /device:TPU:1, one launch (start us, length us, event | category | flops | bytes accessed | tf_op | source)
XLA Modules:
  0.0 91.7 jit_solution(1407473855910457127)
XLA Ops:
  0.6 2.3 %sides.1 = (bf16[3,2,128,128]{3,2,1,0:T(8,128)(2,1)S(1)}, bf16[3,2,128,128]{3,2,1,0:T(8,128)(2,1)}) custom-call(bf16[2,128,2,24,128]{4,3,2,1,0:T(8,128)(2,1)} %velocity.5), custom_call_target="tpu_custom_call" | custom-call | tf_op jit(solution)/shard_map/sides/pallas_call | solution.py:284
  2.9 1.3 %span.1 = (bf16[8,6144]{1,0:T(8,128)(2,1)}, bf16[8,6144]{1,0:T(8,128)(2,1)}, bf16[3,2,128,128]{3,2,1,0:T(8,128)(2,1)}) custom-call(bf16[2,128,2,24,128]{4,3,2,1,0:T(8,128)(2,1)S(1)} %copy-done, bf16[3,2,128,128]{3,2,1,0:T(8,128)(2,1)S(1)} %get-tuple-element.11.passed), custom_call_target="tpu_custom_call" | custom-call | tf_op jit(solution)/shard_map/span/pallas_call | solution.py:284
  4.2 4.8 %collective-permute-start = (bf16[8,6144]{1,0:T(8,128)(2,1)}, bf16[8,6144]{1,0:T(8,128)(2,1)}, u32[]{:S(2)}, u32[]{:S(2)}) collective-permute-start(bf16[8,6144]{1,0:T(8,128)(2,1)} %get-tuple-element.12), channel_id=1, source_target_pairs={{0,1},{1,2},{2,3},{3,4},{4,5},{5,6},{6,7},{7,8},{8,9},{9,10},{10,1... | collective-permute-start | bytes 294920 | tf_op jit(solution)/shard_map/ppermute | solution.py:262
  9.0 12.2 %collective-permute-start.1 = (bf16[8,6144]{1,0:T(8,128)(2,1)}, bf16[8,6144]{1,0:T(8,128)(2,1)}, u32[]{:S(2)}, u32[]{:S(2)}) collective-permute-start(bf16[8,6144]{1,0:T(8,128)(2,1)} %get-tuple-element.13), channel_id=1, source_target_pairs={{0,11},{1,0},{2,1},{3,2},{4,3},{5,4},{6,5},{7,6},{8,7},{9,8},{10,9... | collective-permute-start | bytes 294920 | tf_op jit(solution)/shard_map/ppermute | solution.py:262
  21.2 2.9 %collective-permute-start.3 = (bf16[3,2,128,128]{3,2,1,0:T(8,128)(2,1)}, bf16[3,2,128,128]{3,2,1,0:T(8,128)(2,1)S(1)}, u32[]{:S(2)}, u32[]{:S(2)}) collective-permute-start(bf16[3,2,128,128]{3,2,1,0:T(8,128)(2,1)} %get-tuple-element.15), channel_id=1, source_target_pairs={{0,756},{12,0},{24,12},{36,24},{48,36},{60,48},{72,60},{84,72},{96... | collective-permute-start | bytes 589832 | tf_op jit(solution)/shard_map/ppermute | solution.py:262
  24.1 3.0 %collective-permute-start.2 = (bf16[3,2,128,128]{3,2,1,0:T(8,128)(2,1)}, bf16[3,2,128,128]{3,2,1,0:T(8,128)(2,1)S(1)}, u32[]{:S(2)}, u32[]{:S(2)}) collective-permute-start(bf16[3,2,128,128]{3,2,1,0:T(8,128)(2,1)} %get-tuple-element.14), channel_id=1, source_target_pairs={{0,12},{12,24},{24,36},{36,48},{48,60},{60,72},{72,84},{84,96},{96... | collective-permute-start | bytes 589832 | tf_op jit(solution)/shard_map/ppermute | solution.py:262
  27.2 1.0 %inner.1 = f32[6144,128]{1,0:T(8,128)S(1)} custom-call(bf16[2,128,2,24,128]{4,3,2,1,0:T(8,128)(2,1)S(1)} %copy-done), custom_call_target="tpu_custom_call" | custom-call | tf_op jit(solution)/shard_map/inner/pallas_call | solution.py:284
  28.2 0.0 collective-permute-done.left_u
  28.2 0.0 collective-permute-done.1.right_u
  28.2 1.6 %across.1.inner = f32[6144,128]{1,0:T(8,128)S(1)} custom-call(f32[6144,128]{1,0:T(8,128)S(1)} %inner.1, bf16[8,6144]{1,0:T(8,128)(2,1)} %collective-permute-done.left_u, bf16[8,6144]{1,0:T(8,128)(2,1)} %collective-permute-done.1.right_u), custom_call_target="tpu_custom_call" | custom-call | tf_op jit(solution)/shard_map/across/pallas_call | solution.py:284
  29.8 0.0 copy-start.1
  29.8 0.0 copy-start.2
  29.8 2.2 %collective-permute-done.2.left_w = bf16[3,2,128,128]{3,2,1,0:T(8,128)(2,1)S(1)} collective-permute-done((bf16[3,2,128,128]{3,2,1,0:T(8,128)(2,1)}, bf16[3,2,128,128]{3,2,1,0:T(8,128)(2,1)S(1)}, u32[]{:S(2)}, u32[]{:S(2)}) %collective-permute-start.2) | collective-permute-done | bytes 196640 | tf_op jit(solution)/shard_map/ppermute | solution.py:262
  32.0 1.7 %gram.1 = (bf16[48,128,128]{2,1,0:T(8,128)(2,1)S(1)}, f32[64,1,384]{2,1,0:T(1,128)S(1)}) custom-call(f32[6144,128]{1,0:T(8,128)S(1)} %across.1.inner, bf16[3,2,128,128]{3,2,1,0:T(8,128)(2,1)S(1)} %collective-permute-done.2.left_w, bf16[3,2,128,128]{3,2,1,0:T(8,128)(2,1)S(1)} %collective-permute-done.3.right_w, s32[1,64]{1,0:T(1,128)S(1)} %fusion.1.place), custom_call_target="tpu_custom_call" | custom-call | tf_op jit(solution)/shard_map/gram/pallas_call | solution.py:284
  33.7 18.1 %all_to_all.15 = f32[64,1,384]{2,1,0:T(1,128)S(1)} all-to-all(f32[64,1,384]{2,1,0:T(1,128)S(1)} %get-tuple-element.16), channel_id=1, replica_groups=mesh['chips'=32,'cores'=2,'gz'=12] {'chips'}, dimensions={0} | all-to-all | bytes 196608 | tf_op jit(solution)/shard_map/all_to_all | solution.py:266
  51.8 0.2 reduce.2
  52.0 0.1 reshape.26
  52.1 0.1 reduce_sum.18
  52.2 0.1 tile.9
  52.3 18.0 %all_to_all.16 = f32[48,1,384]{2,1,0:T(1,128)S(1)} all-to-all(f32[48,1,384]{2,1,0:T(1,128)S(1)} %tile.9), channel_id=1, replica_groups=mesh['chips'=32,'cores'=2,'gz'=12] {'cores','gz'}, dimensions={0} | all-to-all | bytes 147456 | tf_op jit(solution)/shard_map/all_to_all | solution.py:266
  70.3 0.2 reduce.3
  70.6 0.1 tile.21
  70.7 12.1 %all_to_all.17.rows = f32[64,1,384]{2,1,0:T(1,128)S(1)} all-to-all(f32[64,1,384]{2,1,0:T(1,128)S(1)} %tile.21), channel_id=1, replica_groups=mesh['chips'=32,'cores'=2,'gz'=12] {'chips'}, dimensions={0} | all-to-all | bytes 196608 | tf_op jit(solution)/shard_map/all_to_all | solution.py:266
  82.8 8.8 %modes.1 = (bf16[64,2,24,128]{3,2,1,0:T(8,128)(2,1)}, f32[64,128]{1,0:T(8,128)}) custom-call(f32[64,1,384]{2,1,0:T(1,128)S(1)} %all_to_all.17.rows, s32[1,128]{1,0:T(1,128)S(1)} %bitcast.6, f32[64,128]{1,0:T(8,128)S(1)} %bitcast.5, bf16[48,128,128]{2,1,0:T(8,128)(2,1)S(1)} %get-tuple-element.17.vort), custom_call_target="tpu_custom_call" | custom-call | tf_op jit(solution)/shard_map/modes/pallas_call | solution.py:284
  (12 shorter events, 0.2 us)
Async XLA Ops:
  0.6 2.3 %copy-start = (bf16[2,128,2,24,128]{4,3,2,1,0:T(8,128)(2,1)S(1)}, bf16[2,128,2,24,128]{4,3,2,1,0:T(8,128)(2,1)}, u32[]{:S(2)}) copy-start(bf16[2,128,2,24,128]{4,3,2,1,0:T(8,128)(2,1)} %velocity.5) | copy-start | bytes 9437188
  0.6 26.5 %copy-start.3 = (s32[64]{0:T(128)S(1)}, s32[64]{0:T(128)}, u32[]{:S(2)}) copy-start(s32[64]{0:T(128)} %param.6) | copy-start | bytes 772
  4.2 24.0 %collective-permute-start = (bf16[8,6144]{1,0:T(8,128)(2,1)}, bf16[8,6144]{1,0:T(8,128)(2,1)}, u32[]{:S(2)}, u32[]{:S(2)}) collective-permute-start(bf16[8,6144]{1,0:T(8,128)(2,1)} %get-tuple-element.12), channel_id=1, source_target_pairs={{0,1},{1,2},{2,3},{3,4},{4,5},{5,6},{6,7},{7,8},{8,9},{9,10},{10,1... | collective-permute-start | bytes 294920 | tf_op jit(solution)/shard_map/ppermute | solution.py:262
  9.0 19.2 %collective-permute-start.1 = (bf16[8,6144]{1,0:T(8,128)(2,1)}, bf16[8,6144]{1,0:T(8,128)(2,1)}, u32[]{:S(2)}, u32[]{:S(2)}) collective-permute-start(bf16[8,6144]{1,0:T(8,128)(2,1)} %get-tuple-element.13), channel_id=1, source_target_pairs={{0,11},{1,0},{2,1},{3,2},{4,3},{5,4},{6,5},{7,6},{8,7},{9,8},{10,9... | collective-permute-start | bytes 294920 | tf_op jit(solution)/shard_map/ppermute | solution.py:262
  21.2 8.6 %collective-permute-start.3 = (bf16[3,2,128,128]{3,2,1,0:T(8,128)(2,1)}, bf16[3,2,128,128]{3,2,1,0:T(8,128)(2,1)S(1)}, u32[]{:S(2)}, u32[]{:S(2)}) collective-permute-start(bf16[3,2,128,128]{3,2,1,0:T(8,128)(2,1)} %get-tuple-element.15), channel_id=1, source_target_pairs={{0,756},{12,0},{24,12},{36,24},{48,36},{60,48},{72,60},{84,72},{96... | collective-permute-start | bytes 589832 | tf_op jit(solution)/shard_map/ppermute | solution.py:262
  24.1 7.9 %collective-permute-start.2 = (bf16[3,2,128,128]{3,2,1,0:T(8,128)(2,1)}, bf16[3,2,128,128]{3,2,1,0:T(8,128)(2,1)S(1)}, u32[]{:S(2)}, u32[]{:S(2)}) collective-permute-start(bf16[3,2,128,128]{3,2,1,0:T(8,128)(2,1)} %get-tuple-element.14), channel_id=1, source_target_pairs={{0,12},{12,24},{24,36},{36,48},{48,60},{60,72},{72,84},{84,96},{96... | collective-permute-start | bytes 589832 | tf_op jit(solution)/shard_map/ppermute | solution.py:262
  29.8 53.1 %copy-start.1 = (f32[128,64]{0,1:T(8,128)S(1)}, f32[128,64]{0,1:T(8,128)}, u32[]{:S(2)}) copy-start(f32[128,64]{0,1:T(8,128)} %param.7) | copy-start | bytes 98308
  29.8 53.0 %copy-start.2 = (s32[128]{0:T(128)S(1)}, s32[128]{0:T(128)}, u32[]{:S(2)}) copy-start(s32[128]{0:T(128)} %param.5) | copy-start | bytes 1540

commit v5 on v4

--- a/solution.py
+++ b/solution.py
@@ -19,6 +19,7 @@
 GROUP = 8
 FEW = 4
 PIECES = 16
+LOADS = 2
 KERNEL_VMEM = 16 << 20
 HIGHEST = lax.Precision.HIGHEST
 NT = (((1,), (1,)), ((), ()))
@@ -84,57 +85,59 @@
     return lax.dot_general(left, right, dims, preferred_element_type=jnp.float32)
 
 
-def flat_rows(velocity, field, start, count):
-    block = velocity[field, start : start + count]
+def flat_rows(field, start, count):
+    block = field[start : start + count]
     return block.reshape(-1, block.shape[-1])
 
 
-def two_blocks(velocity, field, start):
-    blocks = [flat_rows(velocity, field, start + at, FEW) for at in (0, FEW)]
-    return jnp.concatenate(blocks, axis=1)
-
-
-def sides_kernel(velocity, head, tail, first, last, first_rows, last_rows, landed):
-    reach, planes, snaps, cols_z = head.shape
-    cols_x = velocity.shape[3]
-    first_copy = pltpu.make_async_copy(velocity.at[1, :, :, pl.ds(0, GROUP)], first, landed.at[0])
-    last_copy = pltpu.make_async_copy(velocity.at[1, :, :, pl.ds(cols_x - GROUP, GROUP)], last, landed.at[1])
-    first_copy.start()
-    last_copy.start()
+def two_blocks(field, start):
+    return jnp.concatenate([flat_rows(field, start + at, FEW) for at in (0, FEW)], axis=1)
+
+
+def ends_kernel(velocity, head_w, tail_w, head_u, tail_u, wide, long, first_rows, last_rows, landed):
+    reach, planes, snaps, cols_z = head_w.shape
+    cols_x = wide.shape[2]
+    share = snaps // LOADS
+    loads = []
+    for field, near_field in ((1, wide), (0, long)):
+        for part in range(LOADS):
+            here = pl.ds(part * share, share)
+            source = velocity.at[field, here]
+            loads.append(pltpu.make_async_copy(source, near_field.at[here], landed.at[len(loads)]))
+            loads[-1].start()
     stride = planes * GROUP
-    last_start = GROUP - reach
-    for copy, tiles, rows, side, start in (
-        (first_copy, first, first_rows, head, 0),
-        (last_copy, last, last_rows, tail, last_start),
-    ):
-        copy.wait()
-        rows[...] = tiles[...].reshape(rows.shape).astype(jnp.float32)
+    for part in range(LOADS):
+        loads[part].wait()
+        here = slice(part * share, (part + 1) * share)
+        rows = slice(part * share * stride, (part + 1) * share * stride)
+        size = (share * stride, cols_z)
+        first_rows[rows, :] = wide[here, :, :GROUP].reshape(size).astype(jnp.float32)
+        last_rows[rows, :] = wide[here, :, cols_x - GROUP :].reshape(size).astype(jnp.float32)
         for p in range(planes):
             for h in range(reach):
-                at = p * GROUP + start + h
-                side[h, p] = rows[pl.ds(at, snaps, stride=stride), :].astype(jnp.bfloat16)
-
-
-def span_kernel(velocity, passed, head, tail, passed_on):
-    snaps, planes, cols_x = velocity.shape[1:4]
-    share = 2 * GROUP
-    ends_z = ends_z_table(velocity.shape[4])
-    passed_on[...] = passed[...]
-    for start in range(0, snaps, share):
-        span = slice(start * planes * cols_x, (start + share) * planes * cols_x)
-        cols = matmul(ends_z, flat_rows(velocity, 0, start, share), NT).astype(jnp.bfloat16)
-        head[:, span] = cols[:GROUP]
-        tail[:, span] = cols[GROUP:]
-
-
-def inner_kernel(velocity, out):
-    planes, cols_x, cols_z = velocity.shape[2:]
+                at = part * share * stride + p * GROUP + h
+                head_w[h, p, here, :] = first_rows[pl.ds(at, share, stride=stride), :].astype(jnp.bfloat16)
+                at = at + GROUP - reach
+                tail_w[h, p, here, :] = last_rows[pl.ds(at, share, stride=stride), :].astype(jnp.bfloat16)
+    ends_z = ends_z_table(cols_z)
+    few = 2 * GROUP
+    for part in range(LOADS):
+        loads[LOADS + part].wait()
+        for start in range(part * share, (part + 1) * share, few):
+            span = slice(start * planes * cols_x, (start + few) * planes * cols_x)
+            cols = matmul(ends_z, flat_rows(long, start, few), NT).astype(jnp.bfloat16)
+            head_u[:, span] = cols[:GROUP]
+            tail_u[:, span] = cols[GROUP:]
+
+
+def inner_kernel(long, wide, out):
+    planes, cols_x, cols_z = wide.shape[1:]
     count = FEW * planes * cols_x
     along_x = along_x_table(FEW * planes, cols_x)
     along_z = along_z_table(cols_z)
-    for q in range(velocity.shape[1] // (2 * FEW)):
-        value = matmul(along_x, two_blocks(velocity, 1, 2 * FEW * q))
-        value = value + matmul(two_blocks(velocity, 0, 2 * FEW * q), along_z)
+    for q in range(wide.shape[0] // (2 * FEW)):
+        value = matmul(along_x, two_blocks(wide, 2 * FEW * q))
+        value = value + matmul(two_blocks(long, 2 * FEW * q), along_z)
         for half in range(2):
             at = (2 * q + half) * count
             out[at : at + count, :] = value[:, half * cols_z : (half + 1) * cols_z]
@@ -152,30 +155,59 @@
             out[spans[half], :] = inner[spans[half], :] + value[:, half * cols_z : (half + 1) * cols_z]
 
 
-def gram_kernel(inner, left_w, right_w, place, vort, rows_out):
-    lines, snaps, cols_z = vort.shape
+def inside_lines(planes, cols_x):
+    return [p * cols_x + x for p in range(planes) for x in range(REACH, cols_x - REACH)]
+
+
+def outside_lines(planes, cols_x):
+    inside = set(inside_lines(planes, cols_x))
+    return [line for line in range(planes * cols_x) if line not in inside]
+
+
+def gram_of(lines, vorticity, place, vort):
+    _, snaps, cols_z = vort.shape
+    kept = place.shape[1]
+    gram = jnp.zeros((snaps + kept, snaps), jnp.float32)
+    lane = index((kept, 2 * cols_z), 1)
+    down = jnp.broadcast_to(place[...].astype(jnp.float32), (GROUP, kept)).T[:, :1]
+    for at in range(0, len(lines), 2):
+        both = []
+        for line in lines[at : at + 2]:
+            value = (vorticity(line) * (1.0 / TAP_SUM)).astype(jnp.bfloat16)
+            vort[at + len(both)] = value
+            both.append(value)
+        both = jnp.concatenate(both, axis=1)
+        cell = lane + jnp.where(lane < cols_z, lines[at] * cols_z, (lines[at + 1] - 1) * cols_z)
+        chosen = jnp.where(cell.astype(jnp.float32) == down, 1.0, 0.0).astype(jnp.bfloat16)
+        gram = gram + matmul(jnp.concatenate([both, chosen], axis=0), both, NT)
+    return gram
+
+
+def inside_kernel(planes, inner, place, vort, partial_gram):
+    snaps = vort.shape[1]
+    lines = inner.shape[0] // snaps
+    vorticity = lambda line: inner[pl.ds(line, snaps, stride=lines), :]
+    partial_gram[...] = gram_of(inside_lines(planes, lines // planes), vorticity, place, vort)
+
+
+def outside_kernel(inner, left_w, right_w, place, partial_gram, vort, rows_out):
+    snaps = vort.shape[1]
     planes = left_w.shape[1]
+    lines = inner.shape[0] // snaps
     cols_x = lines // planes
     kept = place.shape[1]
-    gram = jnp.zeros((snaps + kept, snaps), jnp.float32)
-    lane = lax.broadcasted_iota(jnp.int32, (kept, 2 * cols_z), 1).astype(jnp.float32)
-    down = jnp.broadcast_to(place[...].astype(jnp.float32), (GROUP, kept)).T[:, :1]
-    for pair in range(lines // 2):
-        sides = []
-        for line in (2 * pair, 2 * pair + 1):
-            p, x = line // cols_x, line % cols_x
-            value = inner[pl.ds(line, snaps, stride=lines), :]
-            for h in range(REACH):
-                if tap(cols_x + h - x):
-                    value = value + tap(cols_x + h - x) * right_w[h, p].astype(jnp.float32)
-                if tap(h - REACH - x):
-                    value = value + tap(h - REACH - x) * left_w[h, p].astype(jnp.float32)
-            value = (value * (1.0 / TAP_SUM)).astype(jnp.bfloat16)
-            vort[line] = value
-            sides.append(value)
-        both = jnp.concatenate(sides, axis=1)
-        chosen = jnp.where(lane == down - float(2 * pair * cols_z), 1.0, 0.0).astype(jnp.bfloat16)
-        gram = gram + matmul(jnp.concatenate([both, chosen], axis=0), both, NT)
+
+    def vorticity(line):
+        p, x = line // cols_x, line % cols_x
+        value = inner[pl.ds(line, snaps, stride=lines), :]
+        for h in range(REACH):
+            if tap(cols_x + h - x):
+                value = value + tap(cols_x + h - x) * right_w[h, p].astype(jnp.float32)
+            if tap(h - REACH - x):
+                value = value + tap(h - REACH - x) * left_w[h, p].astype(jnp.float32)
+        return value
+
+    gram = partial_gram[...] + gram_of(outside_lines(planes, cols_x), vorticity, place, vort)
     for part in range((snaps + kept) // kept):
         rows_out[:, 0, part * snaps : (part + 1) * snaps] = gram[part * kept : (part + 1) * kept]
 
@@ -222,9 +254,10 @@
     return jnp.concatenate(block_rows, axis=0)
 
 
-def modes_kernel(cells, rows, rank, start, vort, modes, basis, work):
+def modes_kernel(cells, rows, rank, start, vort_in, vort_out, modes, basis, work):
     kept, snaps = start.shape
-    lines = vort.shape[0]
+    planes, cols_x = modes.shape[1:3]
+    lines = planes * cols_x
     parts = [rows[:, 0, b * snaps : (b + 1) * snaps] for b in range(snaps // kept + 1)]
     gram = jnp.concatenate(parts[:-1], axis=0) * (1.0 / cells)
     picked = parts[-1]
@@ -239,8 +272,12 @@
     anchor = jnp.sum(picked * coef.astype(jnp.float32), axis=1, keepdims=True)
     orient = anchor / jnp.maximum(jnp.abs(anchor), 1.0)
     basis[...] = now * orient
-    for line in range(lines):
-        work[pl.ds(line, kept, stride=lines), :] = matmul(coef, vort[line]) * orient
+    for vort, held in (
+        (vort_in, inside_lines(planes, cols_x)),
+        (vort_out, outside_lines(planes, cols_x)),
+    ):
+        for at, line in enumerate(held):
+            work[pl.ds(line, kept, stride=lines), :] = matmul(coef, vort[at]) * orient
     modes[...] = work[...].astype(jnp.bfloat16).reshape(modes.shape)
 
 
@@ -303,26 +340,36 @@
     side = near((REACH, planes, snaps, cols_z), jnp.bfloat16)
     strip = near((GROUP, snaps * lines), jnp.bfloat16)
     rows_at = pltpu.VMEM((snaps * planes * GROUP, cols_z), jnp.float32)
-    tiles = pltpu.VMEM((snaps, planes, GROUP, cols_z), jnp.bfloat16)
-    scratch = [tiles, tiles, rows_at, rows_at, pltpu.SemaphoreType.DMA((2,))]
-    head_w, tail_w = local_call(sides_kernel, [side, side], "sides", scratch, pltpu.HBM)(velocity)
+    local = near((snaps, planes, cols_x, cols_z), jnp.bfloat16)
+    head_w, tail_w, head_u, tail_u, wide, long = local_call(
+        ends_kernel,
+        [side, side, strip, strip, local, local],
+        "ends",
+        [rows_at, rows_at, pltpu.SemaphoreType.DMA((2 * LOADS,))],
+        pltpu.HBM,
+    )(velocity)
     left_w = shifted(tail_w, GX, 1)
-    head_u, tail_u, head_w = local_call(span_kernel, [strip, strip, side], "span")(velocity, head_w)
     right_w = shifted(head_w, GX, -1)
     left_u = shifted(tail_u, GZ, 1)
     right_u = shifted(head_u, GZ, -1)
     field = near((snaps * lines, cols_z), jnp.float32)
-    (inner,) = local_call(inner_kernel, [field], "inner")(velocity)
+    (inner,) = local_call(inner_kernel, [field], "inner")(long, wide)
     (inner,) = local_call(across_kernel, [field], "across")(inner, left_u, right_u)
     place = local_place(anchor_index, planes, cols_x, cols_z, total_x, total_z)
-    vort, rows = local_call(
-        gram_kernel,
+    within = len(inside_lines(planes, cols_x))
+    vort_in, partial_gram = local_call(
+        partial(inside_kernel, planes),
+        [near((within, snaps, cols_z), jnp.bfloat16), near((snaps + kept, snaps), jnp.float32)],
+        "inside",
+    )(inner, place[None, :])
+    vort_out, rows = local_call(
+        outside_kernel,
         [
-            near((lines, snaps, cols_z), jnp.bfloat16),
+            near((lines - within, snaps, cols_z), jnp.bfloat16),
             near((kept, 1, (snaps // kept + 1) * snaps), jnp.float32),
         ],
-        "gram",
-    )(inner, left_w, right_w, place[None, :])
+        "outside",
+    )(inner, left_w, right_w, place[None, :], partial_gram)
     mine = summed(exchanged(rows, CHIPS), CHIPS)
     mine = summed(exchanged(copies(mine, (CORES, GZ)), (CORES, GZ)), (CORES, GZ))
     rows = exchanged(copies(mine, CHIPS), CHIPS)
@@ -334,7 +381,7 @@
         ],
         "modes",
         [pltpu.VMEM((kept * lines, cols_z), jnp.float32)],
-    )(rows, snapshot_rank[None, :], start_basis.T, vort)
+    )(rows, snapshot_rank[None, :], start_basis.T, vort_in, vort_out)
     return modes, basis.T
 
 

time: 92.4 us -> 90.3 us (0.977)
  blocking collectives: 48.2 us -> 47.1 us
    all_to_all x3, blocking collectives: 48.2 us -> 47.1 us  [exchanged(): return lax.all_to_all(rows, axis, 0, 0, tiled=True)]
  transfers between devices with their start and end apart: 4 -> 4, of which waited for: 1 -> 1; matrix products, arithmetic and copies ran while one was open for 0% -> 0% of each run, Pallas kernels for 3% -> 4%
where the time goes in v5:
time: 90.3 us; the launch traced here: 89.4 us
  blocking collectives  47.1 us (52%)
  starting transfers between devices  22.9 us (25%)
  Pallas kernels  16.2 us (18%)
  waiting for transfers between devices  1.37 us (2%)
    all_to_all x3, blocking collectives, exchanged(): return lax.all_to_all(rows, axis, 0, 0, tiled=True)  47.1 us
    ppermute x4, starting transfers between devices, shifted(): lax.ppermute(value, axis, [(i, (i + step) % count) for i in range(count)])  22.9 us
    pallas_call x6, Pallas kernels, run(): pl.pallas_call(kernel, in_specs=[pl.BlockSpec(memory_space=space)] * len(...  16.2 us
  transfers between devices with their start and end apart: 4, of which 1 were waited for; matrix products, arithmetic and copies ran while one was open for 0% of the time, Pallas kernels for 4%

profile of v5, /device:TPU:1, one launch (start us, length us, event | category | flops | bytes accessed | tf_op | source)
XLA Modules:
  0.0 89.4 jit_solution(13786900241064373688)
XLA Ops:
  0.6 3.0 %ends.1 = (bf16[3,2,128,128]{3,2,1,0:T(8,128)(2,1)}, bf16[3,2,128,128]{3,2,1,0:T(8,128)(2,1)}, bf16[8,6144]{1,0:T(8,128)(2,1)}, bf16[8,6144]{1,0:T(8,128)(2,1)},...) custom-call(bf16[2,128,2,24,128]{4,3,2,1,0:T(8,128)(2,1)} %velocity.1), custom_call_target="tpu_custom_call" | custom-call | tf_op jit(solution)/shard_map/ends/pallas_call | solution.py:321
  3.6 4.8 %collective-permute-start = (bf16[8,6144]{1,0:T(8,128)(2,1)}, bf16[8,6144]{1,0:T(8,128)(2,1)}, u32[]{:S(2)}, u32[]{:S(2)}) collective-permute-start(bf16[8,6144]{1,0:T(8,128)(2,1)} %get-tuple-element.16), channel_id=1, source_target_pairs={{0,1},{1,2},{2,3},{3,4},{4,5},{5,6},{6,7},{7,8},{8,9},{9,10},{10,1... | collective-permute-start | bytes 294920 | tf_op jit(solution)/shard_map/ppermute | solution.py:299
  8.5 12.2 %collective-permute-start.1 = (bf16[8,6144]{1,0:T(8,128)(2,1)}, bf16[8,6144]{1,0:T(8,128)(2,1)}, u32[]{:S(2)}, u32[]{:S(2)}) collective-permute-start(bf16[8,6144]{1,0:T(8,128)(2,1)} %get-tuple-element.17), channel_id=1, source_target_pairs={{0,11},{1,0},{2,1},{3,2},{4,3},{5,4},{6,5},{7,6},{8,7},{9,8},{10,9... | collective-permute-start | bytes 294920 | tf_op jit(solution)/shard_map/ppermute | solution.py:299
  20.7 4.0 %collective-permute-start.2 = (bf16[3,2,128,128]{3,2,1,0:T(8,128)(2,1)}, bf16[3,2,128,128]{3,2,1,0:T(8,128)(2,1)S(1)}, u32[]{:S(2)}, u32[]{:S(2)}) collective-permute-start(bf16[3,2,128,128]{3,2,1,0:T(8,128)(2,1)} %get-tuple-element.18), channel_id=1, source_target_pairs={{0,12},{12,24},{24,36},{36,48},{48,60},{60,72},{72,84},{84,96},{96... | collective-permute-start | bytes 589832 | tf_op jit(solution)/shard_map/ppermute | solution.py:299
  24.7 1.9 %collective-permute-start.3 = (bf16[3,2,128,128]{3,2,1,0:T(8,128)(2,1)}, bf16[3,2,128,128]{3,2,1,0:T(8,128)(2,1)S(1)}, u32[]{:S(2)}, u32[]{:S(2)}) collective-permute-start(bf16[3,2,128,128]{3,2,1,0:T(8,128)(2,1)} %get-tuple-element.19), channel_id=1, source_target_pairs={{0,756},{12,0},{24,12},{36,24},{48,36},{60,48},{72,60},{84,72},{96... | collective-permute-start | bytes 589832 | tf_op jit(solution)/shard_map/ppermute | solution.py:299
  26.6 1.0 %inner.1 = f32[6144,128]{1,0:T(8,128)S(1)} custom-call(bf16[128,2,24,128]{3,2,1,0:T(8,128)(2,1)S(1)} %get-tuple-element.14.long, bf16[128,2,24,128]{3,2,1,0:T(8,128)(2,1)S(1)} %get-tuple-element.15.wide), custom_call_target="tpu_custom_call" | custom-call | tf_op jit(solution)/shard_map/inner/pallas_call | solution.py:321
  27.6 0.0 collective-permute-done.left_u
  27.7 0.0 collective-permute-done.1.right_u
  27.7 1.6 %across.1.inner = f32[6144,128]{1,0:T(8,128)S(1)} custom-call(f32[6144,128]{1,0:T(8,128)S(1)} %inner.1, bf16[8,6144]{1,0:T(8,128)(2,1)} %collective-permute-done.left_u, bf16[8,6144]{1,0:T(8,128)(2,1)} %collective-permute-done.1.right_u), custom_call_target="tpu_custom_call" | custom-call | tf_op jit(solution)/shard_map/across/pallas_call | solution.py:321
  29.2 1.2 %inside.1 = (bf16[36,128,128]{2,1,0:T(8,128)(2,1)S(1)}, f32[192,128]{1,0:T(8,128)S(1)}) custom-call(f32[6144,128]{1,0:T(8,128)S(1)} %across.1.inner, s32[1,64]{1,0:T(1,128)S(1)} %fusion.1.place), custom_call_target="tpu_custom_call" | custom-call | tf_op jit(solution)/shard_map/inside/pallas_call | solution.py:321
  30.5 0.0 copy-start
  30.5 0.0 copy-start.1
  30.5 1.4 %collective-permute-done.3.right_w = bf16[3,2,128,128]{3,2,1,0:T(8,128)(2,1)S(1)} collective-permute-done((bf16[3,2,128,128]{3,2,1,0:T(8,128)(2,1)}, bf16[3,2,128,128]{3,2,1,0:T(8,128)(2,1)S(1)}, u32[]{:S(2)}, u32[]{:S(2)}) %collective-permute-start.3) | collective-permute-done | bytes 196640 | tf_op jit(solution)/shard_map/ppermute | solution.py:299
  31.9 0.6 outside.1
  32.5 20.6 %all_to_all.15 = f32[64,1,384]{2,1,0:T(1,128)S(1)} all-to-all(f32[64,1,384]{2,1,0:T(1,128)S(1)} %get-tuple-element.21), channel_id=1, replica_groups=mesh['chips'=32,'cores'=2,'gz'=12] {'chips'}, dimensions={0} | all-to-all | bytes 196608 | tf_op jit(solution)/shard_map/all_to_all | solution.py:303
  53.1 0.2 reduce.2
  53.3 0.1 reshape.26
  53.4 0.1 reduce_sum.18
  53.5 0.1 tile.9
  53.6 14.5 %all_to_all.16 = f32[48,1,384]{2,1,0:T(1,128)S(1)} all-to-all(f32[48,1,384]{2,1,0:T(1,128)S(1)} %tile.9), channel_id=1, replica_groups=mesh['chips'=32,'cores'=2,'gz'=12] {'cores','gz'}, dimensions={0} | all-to-all | bytes 147456 | tf_op jit(solution)/shard_map/all_to_all | solution.py:303
  68.1 0.2 reduce.3
  68.4 0.1 tile.21
  68.5 12.0 %all_to_all.17.rows = f32[64,1,384]{2,1,0:T(1,128)S(1)} all-to-all(f32[64,1,384]{2,1,0:T(1,128)S(1)} %tile.21), channel_id=1, replica_groups=mesh['chips'=32,'cores'=2,'gz'=12] {'chips'}, dimensions={0} | all-to-all | bytes 196608 | tf_op jit(solution)/shard_map/all_to_all | solution.py:303
  80.6 8.8 %modes.1 = (bf16[64,2,24,128]{3,2,1,0:T(8,128)(2,1)}, f32[64,128]{1,0:T(8,128)}) custom-call(f32[64,1,384]{2,1,0:T(1,128)S(1)} %all_to_all.17.rows, s32[1,128]{1,0:T(1,128)S(1)} %bitcast.6, f32[64,128]{1,0:T(8,128)S(1)} %bitcast.5, bf16[36,128,128]{2,1,0:T(8,128)(2,1)S(1)} %get-tuple-element.22.vort_in, bf16[12,128,128]{2,1,0:T(8,128)(2,1)S(1)} %get-tuple-element.23.vort_out), custom_call_target="tpu_custom_call" | custom-call | tf_op jit(solution)/shard_map/modes/pallas_call | solution.py:321
  (10 shorter events, 0.2 us)
Async XLA Ops:
  0.6 26.0 %copy-start.2 = (s32[64]{0:T(128)S(1)}, s32[64]{0:T(128)}, u32[]{:S(2)}) copy-start(s32[64]{0:T(128)} %param.6) | copy-start | bytes 772
  3.6 24.0 %collective-permute-start = (bf16[8,6144]{1,0:T(8,128)(2,1)}, bf16[8,6144]{1,0:T(8,128)(2,1)}, u32[]{:S(2)}, u32[]{:S(2)}) collective-permute-start(bf16[8,6144]{1,0:T(8,128)(2,1)} %get-tuple-element.16), channel_id=1, source_target_pairs={{0,1},{1,2},{2,3},{3,4},{4,5},{5,6},{6,7},{7,8},{8,9},{9,10},{10,1... | collective-permute-start | bytes 294920 | tf_op jit(solution)/shard_map/ppermute | solution.py:299
  8.5 19.2 %collective-permute-start.1 = (bf16[8,6144]{1,0:T(8,128)(2,1)}, bf16[8,6144]{1,0:T(8,128)(2,1)}, u32[]{:S(2)}, u32[]{:S(2)}) collective-permute-start(bf16[8,6144]{1,0:T(8,128)(2,1)} %get-tuple-element.17), channel_id=1, source_target_pairs={{0,11},{1,0},{2,1},{3,2},{4,3},{5,4},{6,5},{7,6},{8,7},{9,8},{10,9... | collective-permute-start | bytes 294920 | tf_op jit(solution)/shard_map/ppermute | solution.py:299
  20.7 9.8 %collective-permute-start.2 = (bf16[3,2,128,128]{3,2,1,0:T(8,128)(2,1)}, bf16[3,2,128,128]{3,2,1,0:T(8,128)(2,1)S(1)}, u32[]{:S(2)}, u32[]{:S(2)}) collective-permute-start(bf16[3,2,128,128]{3,2,1,0:T(8,128)(2,1)} %get-tuple-element.18), channel_id=1, source_target_pairs={{0,12},{12,24},{24,36},{36,48},{48,60},{60,72},{72,84},{84,96},{96... | collective-permute-start | bytes 589832 | tf_op jit(solution)/shard_map/ppermute | solution.py:299
  24.7 7.2 %collective-permute-start.3 = (bf16[3,2,128,128]{3,2,1,0:T(8,128)(2,1)}, bf16[3,2,128,128]{3,2,1,0:T(8,128)(2,1)S(1)}, u32[]{:S(2)}, u32[]{:S(2)}) collective-permute-start(bf16[3,2,128,128]{3,2,1,0:T(8,128)(2,1)} %get-tuple-element.19), channel_id=1, source_target_pairs={{0,756},{12,0},{24,12},{36,24},{48,36},{60,48},{72,60},{84,72},{96... | collective-permute-start | bytes 589832 | tf_op jit(solution)/shard_map/ppermute | solution.py:299
  30.5 50.1 %copy-start = (f32[128,64]{0,1:T(8,128)S(1)}, f32[128,64]{0,1:T(8,128)}, u32[]{:S(2)}) copy-start(f32[128,64]{0,1:T(8,128)} %param.7) | copy-start | bytes 98308
  30.5 50.1 %copy-start.1 = (s32[128]{0:T(128)S(1)}, s32[128]{0:T(128)}, u32[]{:S(2)}) copy-start(s32[128]{0:T(128)} %param.5) | copy-start | bytes 1540

commit v6 on v5

--- a/solution.py
+++ b/solution.py
@@ -303,13 +303,22 @@
     return lax.all_to_all(rows, axis, 0, 0, tiled=True)
 
 
-def summed(rows, axis):
-    count = size_of(axis)
-    return jnp.sum(rows.reshape((count, rows.shape[0] // count) + rows.shape[1:]), axis=0)
-
-
-def copies(rows, axis):
-    return jnp.tile(rows, (size_of(axis),) + (1,) * (rows.ndim - 1))
+def total_kernel(share, rows, out):
+    value = rows[:, 0, :]
+    while value.shape[0] > share:
+        count = value.shape[0] // share
+        if count % 2 == 0:
+            half = value.shape[0] // 2
+            value = value[:half] + value[half:]
+        else:
+            value = sum(value[i * share : (i + 1) * share] for i in range(count))
+    for at in range(0, out.shape[0], share):
+        out[at : at + share, 0, :] = value
+
+
+def totals(rows, share, axes):
+    result = near((share * size_of(axes),) + rows.shape[1:], rows.dtype)
+    return local_call(partial(total_kernel, share), [result], "total")(rows)[0]
 
 
 def near(shape, dtype):
@@ -370,9 +379,10 @@
         ],
         "outside",
     )(inner, left_w, right_w, place[None, :], partial_gram)
-    mine = summed(exchanged(rows, CHIPS), CHIPS)
-    mine = summed(exchanged(copies(mine, (CORES, GZ)), (CORES, GZ)), (CORES, GZ))
-    rows = exchanged(copies(mine, CHIPS), CHIPS)
+    part = kept // size_of(CHIPS)
+    rows = totals(exchanged(rows, CHIPS), part, (CORES, GZ))
+    rows = totals(exchanged(rows, (CORES, GZ)), part, CHIPS)
+    rows = exchanged(rows, CHIPS)
     modes, basis = local_call(
         partial(modes_kernel, float(planes * total_x * total_z)),
         [

time: 90.3 us -> 89.4 us (0.990)
    pallas_call x6 -> x8, Pallas kernels: 16.2 us -> 16.2 us  [run(): pl.pallas_call(kernel, in_specs=[pl.BlockSpec(memory_space=space)] * len(...]
where the time goes in v6:
time: 89.4 us; the launch traced here: 88.5 us
  blocking collectives  47.1 us (53%)
  starting transfers between devices  22.9 us (26%)
  Pallas kernels  16.2 us (18%)
  waiting for transfers between devices  1.39 us (2%)
    all_to_all x3, blocking collectives, exchanged(): return lax.all_to_all(rows, axis, 0, 0, tiled=True)  47.1 us
    ppermute x4, starting transfers between devices, shifted(): lax.ppermute(value, axis, [(i, (i + step) % count) for i in range(count)])  22.9 us
    pallas_call x8, Pallas kernels, run(): pl.pallas_call(kernel, in_specs=[pl.BlockSpec(memory_space=space)] * len(...  16.2 us
  transfers between devices with their start and end apart: 4, of which 1 were waited for; matrix products, arithmetic and copies ran while one was open for 0% of the time, Pallas kernels for 4%

profile of v6, /device:TPU:1, one launch (start us, length us, event | category | flops | bytes accessed | tf_op | source)
XLA Modules:
  0.0 88.5 jit_solution(17124939158183148221)
XLA Ops:
  0.6 0.0 copy-start.2
  0.6 3.0 %ends.1 = (bf16[3,2,128,128]{3,2,1,0:T(8,128)(2,1)}, bf16[3,2,128,128]{3,2,1,0:T(8,128)(2,1)}, bf16[8,6144]{1,0:T(8,128)(2,1)}, bf16[8,6144]{1,0:T(8,128)(2,1)},...) custom-call(bf16[2,128,2,24,128]{4,3,2,1,0:T(8,128)(2,1)} %velocity.1), custom_call_target="tpu_custom_call" | custom-call | tf_op jit(solution)/shard_map/ends/pallas_call | solution.py:330
  3.6 4.8 %collective-permute-start = (bf16[8,6144]{1,0:T(8,128)(2,1)}, bf16[8,6144]{1,0:T(8,128)(2,1)}, u32[]{:S(2)}, u32[]{:S(2)}) collective-permute-start(bf16[8,6144]{1,0:T(8,128)(2,1)} %get-tuple-element.16), channel_id=1, source_target_pairs={{0,1},{1,2},{2,3},{3,4},{4,5},{5,6},{6,7},{7,8},{8,9},{9,10},{10,1... | collective-permute-start | bytes 294920 | tf_op jit(solution)/shard_map/ppermute | solution.py:299
  8.5 12.2 %collective-permute-start.1 = (bf16[8,6144]{1,0:T(8,128)(2,1)}, bf16[8,6144]{1,0:T(8,128)(2,1)}, u32[]{:S(2)}, u32[]{:S(2)}) collective-permute-start(bf16[8,6144]{1,0:T(8,128)(2,1)} %get-tuple-element.17), channel_id=1, source_target_pairs={{0,11},{1,0},{2,1},{3,2},{4,3},{5,4},{6,5},{7,6},{8,7},{9,8},{10,9... | collective-permute-start | bytes 294920 | tf_op jit(solution)/shard_map/ppermute | solution.py:299
  20.7 4.0 %collective-permute-start.2 = (bf16[3,2,128,128]{3,2,1,0:T(8,128)(2,1)}, bf16[3,2,128,128]{3,2,1,0:T(8,128)(2,1)S(1)}, u32[]{:S(2)}, u32[]{:S(2)}) collective-permute-start(bf16[3,2,128,128]{3,2,1,0:T(8,128)(2,1)} %get-tuple-element.18), channel_id=1, source_target_pairs={{0,12},{12,24},{24,36},{36,48},{48,60},{60,72},{72,84},{84,96},{96... | collective-permute-start | bytes 589832 | tf_op jit(solution)/shard_map/ppermute | solution.py:299
  24.7 1.9 %collective-permute-start.3 = (bf16[3,2,128,128]{3,2,1,0:T(8,128)(2,1)}, bf16[3,2,128,128]{3,2,1,0:T(8,128)(2,1)S(1)}, u32[]{:S(2)}, u32[]{:S(2)}) collective-permute-start(bf16[3,2,128,128]{3,2,1,0:T(8,128)(2,1)} %get-tuple-element.19), channel_id=1, source_target_pairs={{0,756},{12,0},{24,12},{36,24},{48,36},{60,48},{72,60},{84,72},{96... | collective-permute-start | bytes 589832 | tf_op jit(solution)/shard_map/ppermute | solution.py:299
  26.6 0.0 copy-done.2
  26.6 1.0 %inner.1 = f32[6144,128]{1,0:T(8,128)S(1)} custom-call(bf16[128,2,24,128]{3,2,1,0:T(8,128)(2,1)S(1)} %get-tuple-element.14.long, bf16[128,2,24,128]{3,2,1,0:T(8,128)(2,1)S(1)} %get-tuple-element.15.wide), custom_call_target="tpu_custom_call" | custom-call | tf_op jit(solution)/shard_map/inner/pallas_call | solution.py:330
  27.6 0.0 collective-permute-done.left_u
  27.7 0.0 collective-permute-done.1.right_u
  27.7 1.6 %across.1.inner = f32[6144,128]{1,0:T(8,128)S(1)} custom-call(f32[6144,128]{1,0:T(8,128)S(1)} %inner.1, bf16[8,6144]{1,0:T(8,128)(2,1)} %collective-permute-done.left_u, bf16[8,6144]{1,0:T(8,128)(2,1)} %collective-permute-done.1.right_u), custom_call_target="tpu_custom_call" | custom-call | tf_op jit(solution)/shard_map/across/pallas_call | solution.py:330
  29.2 0.0 copy-start
  29.2 0.0 copy-start.1
  29.3 1.2 %inside.1 = (bf16[36,128,128]{2,1,0:T(8,128)(2,1)S(1)}, f32[192,128]{1,0:T(8,128)S(1)}) custom-call(f32[6144,128]{1,0:T(8,128)S(1)} %across.1.inner, s32[1,64]{1,0:T(1,128)S(1)} %fusion.1.place), custom_call_target="tpu_custom_call" | custom-call | tf_op jit(solution)/shard_map/inside/pallas_call | solution.py:330
  30.5 0.0 collective-permute-done.2.left_w
  30.5 1.4 %collective-permute-done.3.right_w = bf16[3,2,128,128]{3,2,1,0:T(8,128)(2,1)S(1)} collective-permute-done((bf16[3,2,128,128]{3,2,1,0:T(8,128)(2,1)}, bf16[3,2,128,128]{3,2,1,0:T(8,128)(2,1)S(1)}, u32[]{:S(2)}, u32[]{:S(2)}) %collective-permute-start.3) | collective-permute-done | bytes 196640 | tf_op jit(solution)/shard_map/ppermute | solution.py:299
  31.9 0.6 outside.1
  32.5 20.6 %all_to_all.15.rows = f32[64,1,384]{2,1,0:T(1,128)S(1)} all-to-all(f32[64,1,384]{2,1,0:T(1,128)S(1)} %get-tuple-element.21), channel_id=1, replica_groups=mesh['chips'=32,'cores'=2,'gz'=12] {'chips'}, dimensions={0} | all-to-all | bytes 196608 | tf_op jit(solution)/shard_map/all_to_all | solution.py:303
  53.1 14.5 %all_to_all.16.rows = f32[48,1,384]{2,1,0:T(1,128)S(1)} all-to-all(f32[48,1,384]{2,1,0:T(1,128)S(1)} %total.2), channel_id=1, replica_groups=mesh['chips'=32,'cores'=2,'gz'=12] {'cores','gz'}, dimensions={0} | all-to-all | bytes 147456 | tf_op jit(solution)/shard_map/all_to_all | solution.py:303
  67.6 12.0 %all_to_all.17.rows = f32[64,1,384]{2,1,0:T(1,128)S(1)} all-to-all(f32[64,1,384]{2,1,0:T(1,128)S(1)} %total.3), channel_id=1, replica_groups=mesh['chips'=32,'cores'=2,'gz'=12] {'chips'}, dimensions={0} | all-to-all | bytes 196608 | tf_op jit(solution)/shard_map/all_to_all | solution.py:303
  79.6 0.0 copy-done
  79.6 0.0 copy-done.1
  79.6 8.8 %modes.1 = (bf16[64,2,24,128]{3,2,1,0:T(8,128)(2,1)}, f32[64,128]{1,0:T(8,128)}) custom-call(f32[64,1,384]{2,1,0:T(1,128)S(1)} %all_to_all.17.rows, s32[1,128]{1,0:T(1,128)S(1)} %bitcast.6, f32[64,128]{1,0:T(8,128)S(1)} %bitcast.5, bf16[36,128,128]{2,1,0:T(8,128)(2,1)S(1)} %get-tuple-element.22.vort_in, bf16[12,128,128]{2,1,0:T(8,128)(2,1)S(1)} %get-tuple-element.23.vort_out), custom_call_target="tpu_custom_call" | custom-call | tf_op jit(solution)/shard_map/modes/pallas_call | solution.py:330
  (3 shorter events, 0.1 us)
Async XLA Ops:
  0.6 26.0 %copy-start.2 = (s32[64]{0:T(128)S(1)}, s32[64]{0:T(128)}, u32[]{:S(2)}) copy-start(s32[64]{0:T(128)} %param.6) | copy-start | bytes 772
  3.6 24.0 %collective-permute-start = (bf16[8,6144]{1,0:T(8,128)(2,1)}, bf16[8,6144]{1,0:T(8,128)(2,1)}, u32[]{:S(2)}, u32[]{:S(2)}) collective-permute-start(bf16[8,6144]{1,0:T(8,128)(2,1)} %get-tuple-element.16), channel_id=1, source_target_pairs={{0,1},{1,2},{2,3},{3,4},{4,5},{5,6},{6,7},{7,8},{8,9},{9,10},{10,1... | collective-permute-start | bytes 294920 | tf_op jit(solution)/shard_map/ppermute | solution.py:299
  8.5 19.2 %collective-permute-start.1 = (bf16[8,6144]{1,0:T(8,128)(2,1)}, bf16[8,6144]{1,0:T(8,128)(2,1)}, u32[]{:S(2)}, u32[]{:S(2)}) collective-permute-start(bf16[8,6144]{1,0:T(8,128)(2,1)} %get-tuple-element.17), channel_id=1, source_target_pairs={{0,11},{1,0},{2,1},{3,2},{4,3},{5,4},{6,5},{7,6},{8,7},{9,8},{10,9... | collective-permute-start | bytes 294920 | tf_op jit(solution)/shard_map/ppermute | solution.py:299
  20.7 9.8 %collective-permute-start.2 = (bf16[3,2,128,128]{3,2,1,0:T(8,128)(2,1)}, bf16[3,2,128,128]{3,2,1,0:T(8,128)(2,1)S(1)}, u32[]{:S(2)}, u32[]{:S(2)}) collective-permute-start(bf16[3,2,128,128]{3,2,1,0:T(8,128)(2,1)} %get-tuple-element.18), channel_id=1, source_target_pairs={{0,12},{12,24},{24,36},{36,48},{48,60},{60,72},{72,84},{84,96},{96... | collective-permute-start | bytes 589832 | tf_op jit(solution)/shard_map/ppermute | solution.py:299
  24.7 7.2 %collective-permute-start.3 = (bf16[3,2,128,128]{3,2,1,0:T(8,128)(2,1)}, bf16[3,2,128,128]{3,2,1,0:T(8,128)(2,1)S(1)}, u32[]{:S(2)}, u32[]{:S(2)}) collective-permute-start(bf16[3,2,128,128]{3,2,1,0:T(8,128)(2,1)} %get-tuple-element.19), channel_id=1, source_target_pairs={{0,756},{12,0},{24,12},{36,24},{48,36},{60,48},{72,60},{84,72},{96... | collective-permute-start | bytes 589832 | tf_op jit(solution)/shard_map/ppermute | solution.py:299
  29.2 50.4 %copy-start = (f32[128,64]{0,1:T(8,128)S(1)}, f32[128,64]{0,1:T(8,128)}, u32[]{:S(2)}) copy-start(f32[128,64]{0,1:T(8,128)} %param.7) | copy-start | bytes 98308
  29.2 50.4 %copy-start.1 = (s32[128]{0:T(128)S(1)}, s32[128]{0:T(128)}, u32[]{:S(2)}) copy-start(s32[128]{0:T(128)} %param.5) | copy-start | bytes 1540

commit v7 on v6

--- a/solution.py
+++ b/solution.py
@@ -19,7 +19,7 @@
 GROUP = 8
 FEW = 4
 PIECES = 16
-LOADS = 2
+LOADS = 4
 KERNEL_VMEM = 16 << 20
 HIGHEST = lax.Precision.HIGHEST
 NT = (((1,), (1,)), ((), ()))

time: 89.4 us -> 89.5 us (level)
  no operation moved by 1% of the time
where the time goes in v7:
time: 89.5 us; the launch traced here: 88.6 us
  blocking collectives  47.1 us (53%)
  starting transfers between devices  22.9 us (26%)
  Pallas kernels  16.4 us (18%)
  waiting for transfers between devices  1.37 us (2%)
    all_to_all x3, blocking collectives, exchanged(): return lax.all_to_all(rows, axis, 0, 0, tiled=True)  47.1 us
    ppermute x4, starting transfers between devices, shifted(): lax.ppermute(value, axis, [(i, (i + step) % count) for i in range(count)])  22.9 us
    pallas_call x8, Pallas kernels, run(): pl.pallas_call(kernel, in_specs=[pl.BlockSpec(memory_space=space)] * len(...  16.4 us
  transfers between devices with their start and end apart: 4, of which 1 were waited for; matrix products, arithmetic and copies ran while one was open for 0% of the time, Pallas kernels for 4%

profile of v7, /device:TPU:1, one launch (start us, length us, event | category | flops | bytes accessed | tf_op | source)
XLA Modules:
  0.0 88.6 jit_solution(11889051556054667726)
XLA Ops:
  0.6 0.0 copy-start.2
  0.6 3.1 %ends.1 = (bf16[3,2,128,128]{3,2,1,0:T(8,128)(2,1)}, bf16[3,2,128,128]{3,2,1,0:T(8,128)(2,1)}, bf16[8,6144]{1,0:T(8,128)(2,1)}, bf16[8,6144]{1,0:T(8,128)(2,1)},...) custom-call(bf16[2,128,2,24,128]{4,3,2,1,0:T(8,128)(2,1)} %velocity.1), custom_call_target="tpu_custom_call" | custom-call | tf_op jit(solution)/shard_map/ends/pallas_call | solution.py:330
  3.7 4.8 %collective-permute-start = (bf16[8,6144]{1,0:T(8,128)(2,1)}, bf16[8,6144]{1,0:T(8,128)(2,1)}, u32[]{:S(2)}, u32[]{:S(2)}) collective-permute-start(bf16[8,6144]{1,0:T(8,128)(2,1)} %get-tuple-element.16), channel_id=1, source_target_pairs={{0,1},{1,2},{2,3},{3,4},{4,5},{5,6},{6,7},{7,8},{8,9},{9,10},{10,1... | collective-permute-start | bytes 294920 | tf_op jit(solution)/shard_map/ppermute | solution.py:299
  8.6 12.2 %collective-permute-start.1 = (bf16[8,6144]{1,0:T(8,128)(2,1)}, bf16[8,6144]{1,0:T(8,128)(2,1)}, u32[]{:S(2)}, u32[]{:S(2)}) collective-permute-start(bf16[8,6144]{1,0:T(8,128)(2,1)} %get-tuple-element.17), channel_id=1, source_target_pairs={{0,11},{1,0},{2,1},{3,2},{4,3},{5,4},{6,5},{7,6},{8,7},{9,8},{10,9... | collective-permute-start | bytes 294920 | tf_op jit(solution)/shard_map/ppermute | solution.py:299
  20.8 4.0 %collective-permute-start.2 = (bf16[3,2,128,128]{3,2,1,0:T(8,128)(2,1)}, bf16[3,2,128,128]{3,2,1,0:T(8,128)(2,1)S(1)}, u32[]{:S(2)}, u32[]{:S(2)}) collective-permute-start(bf16[3,2,128,128]{3,2,1,0:T(8,128)(2,1)} %get-tuple-element.18), channel_id=1, source_target_pairs={{0,12},{12,24},{24,36},{36,48},{48,60},{60,72},{72,84},{84,96},{96... | collective-permute-start | bytes 589832 | tf_op jit(solution)/shard_map/ppermute | solution.py:299
  24.8 1.9 %collective-permute-start.3 = (bf16[3,2,128,128]{3,2,1,0:T(8,128)(2,1)}, bf16[3,2,128,128]{3,2,1,0:T(8,128)(2,1)S(1)}, u32[]{:S(2)}, u32[]{:S(2)}) collective-permute-start(bf16[3,2,128,128]{3,2,1,0:T(8,128)(2,1)} %get-tuple-element.19), channel_id=1, source_target_pairs={{0,756},{12,0},{24,12},{36,24},{48,36},{60,48},{72,60},{84,72},{96... | collective-permute-start | bytes 589832 | tf_op jit(solution)/shard_map/ppermute | solution.py:299
  26.7 0.0 copy-done.2
  26.8 1.0 %inner.1 = f32[6144,128]{1,0:T(8,128)S(1)} custom-call(bf16[128,2,24,128]{3,2,1,0:T(8,128)(2,1)S(1)} %get-tuple-element.14.long, bf16[128,2,24,128]{3,2,1,0:T(8,128)(2,1)S(1)} %get-tuple-element.15.wide), custom_call_target="tpu_custom_call" | custom-call | tf_op jit(solution)/shard_map/inner/pallas_call | solution.py:330
  27.8 0.0 collective-permute-done.left_u
  27.8 0.0 collective-permute-done.1.right_u
  27.8 1.6 %across.1.inner = f32[6144,128]{1,0:T(8,128)S(1)} custom-call(f32[6144,128]{1,0:T(8,128)S(1)} %inner.1, bf16[8,6144]{1,0:T(8,128)(2,1)} %collective-permute-done.left_u, bf16[8,6144]{1,0:T(8,128)(2,1)} %collective-permute-done.1.right_u), custom_call_target="tpu_custom_call" | custom-call | tf_op jit(solution)/shard_map/across/pallas_call | solution.py:330
  29.4 0.0 copy-start
  29.4 0.0 copy-start.1
  29.4 1.2 %inside.1 = (bf16[36,128,128]{2,1,0:T(8,128)(2,1)S(1)}, f32[192,128]{1,0:T(8,128)S(1)}) custom-call(f32[6144,128]{1,0:T(8,128)S(1)} %across.1.inner, s32[1,64]{1,0:T(1,128)S(1)} %fusion.1.place), custom_call_target="tpu_custom_call" | custom-call | tf_op jit(solution)/shard_map/inside/pallas_call | solution.py:330
  30.6 0.0 collective-permute-done.2.left_w
  30.6 1.4 %collective-permute-done.3.right_w = bf16[3,2,128,128]{3,2,1,0:T(8,128)(2,1)S(1)} collective-permute-done((bf16[3,2,128,128]{3,2,1,0:T(8,128)(2,1)}, bf16[3,2,128,128]{3,2,1,0:T(8,128)(2,1)S(1)}, u32[]{:S(2)}, u32[]{:S(2)}) %collective-permute-start.3) | collective-permute-done | bytes 196640 | tf_op jit(solution)/shard_map/ppermute | solution.py:299
  32.0 0.6 outside.1
  32.6 20.6 %all_to_all.15.rows = f32[64,1,384]{2,1,0:T(1,128)S(1)} all-to-all(f32[64,1,384]{2,1,0:T(1,128)S(1)} %get-tuple-element.21), channel_id=1, replica_groups=mesh['chips'=32,'cores'=2,'gz'=12] {'chips'}, dimensions={0} | all-to-all | bytes 196608 | tf_op jit(solution)/shard_map/all_to_all | solution.py:303
  53.2 14.5 %all_to_all.16.rows = f32[48,1,384]{2,1,0:T(1,128)S(1)} all-to-all(f32[48,1,384]{2,1,0:T(1,128)S(1)} %total.2), channel_id=1, replica_groups=mesh['chips'=32,'cores'=2,'gz'=12] {'cores','gz'}, dimensions={0} | all-to-all | bytes 147456 | tf_op jit(solution)/shard_map/all_to_all | solution.py:303
  67.8 12.0 %all_to_all.17.rows = f32[64,1,384]{2,1,0:T(1,128)S(1)} all-to-all(f32[64,1,384]{2,1,0:T(1,128)S(1)} %total.3), channel_id=1, replica_groups=mesh['chips'=32,'cores'=2,'gz'=12] {'chips'}, dimensions={0} | all-to-all | bytes 196608 | tf_op jit(solution)/shard_map/all_to_all | solution.py:303
  79.8 0.0 copy-done
  79.8 0.0 copy-done.1
  79.8 8.8 %modes.1 = (bf16[64,2,24,128]{3,2,1,0:T(8,128)(2,1)}, f32[64,128]{1,0:T(8,128)}) custom-call(f32[64,1,384]{2,1,0:T(1,128)S(1)} %all_to_all.17.rows, s32[1,128]{1,0:T(1,128)S(1)} %bitcast.6, f32[64,128]{1,0:T(8,128)S(1)} %bitcast.5, bf16[36,128,128]{2,1,0:T(8,128)(2,1)S(1)} %get-tuple-element.22.vort_in, bf16[12,128,128]{2,1,0:T(8,128)(2,1)S(1)} %get-tuple-element.23.vort_out), custom_call_target="tpu_custom_call" | custom-call | tf_op jit(solution)/shard_map/modes/pallas_call | solution.py:330
  (3 shorter events, 0.1 us)
Async XLA Ops:
  0.6 26.1 %copy-start.2 = (s32[64]{0:T(128)S(1)}, s32[64]{0:T(128)}, u32[]{:S(2)}) copy-start(s32[64]{0:T(128)} %param.6) | copy-start | bytes 772
  3.7 24.1 %collective-permute-start = (bf16[8,6144]{1,0:T(8,128)(2,1)}, bf16[8,6144]{1,0:T(8,128)(2,1)}, u32[]{:S(2)}, u32[]{:S(2)}) collective-permute-start(bf16[8,6144]{1,0:T(8,128)(2,1)} %get-tuple-element.16), channel_id=1, source_target_pairs={{0,1},{1,2},{2,3},{3,4},{4,5},{5,6},{6,7},{7,8},{8,9},{9,10},{10,1... | collective-permute-start | bytes 294920 | tf_op jit(solution)/shard_map/ppermute | solution.py:299
  8.6 19.2 %collective-permute-start.1 = (bf16[8,6144]{1,0:T(8,128)(2,1)}, bf16[8,6144]{1,0:T(8,128)(2,1)}, u32[]{:S(2)}, u32[]{:S(2)}) collective-permute-start(bf16[8,6144]{1,0:T(8,128)(2,1)} %get-tuple-element.17), channel_id=1, source_target_pairs={{0,11},{1,0},{2,1},{3,2},{4,3},{5,4},{6,5},{7,6},{8,7},{9,8},{10,9... | collective-permute-start | bytes 294920 | tf_op jit(solution)/shard_map/ppermute | solution.py:299
  20.8 9.8 %collective-permute-start.2 = (bf16[3,2,128,128]{3,2,1,0:T(8,128)(2,1)}, bf16[3,2,128,128]{3,2,1,0:T(8,128)(2,1)S(1)}, u32[]{:S(2)}, u32[]{:S(2)}) collective-permute-start(bf16[3,2,128,128]{3,2,1,0:T(8,128)(2,1)} %get-tuple-element.18), channel_id=1, source_target_pairs={{0,12},{12,24},{24,36},{36,48},{48,60},{60,72},{72,84},{84,96},{96... | collective-permute-start | bytes 589832 | tf_op jit(solution)/shard_map/ppermute | solution.py:299
  24.8 7.2 %collective-permute-start.3 = (bf16[3,2,128,128]{3,2,1,0:T(8,128)(2,1)}, bf16[3,2,128,128]{3,2,1,0:T(8,128)(2,1)S(1)}, u32[]{:S(2)}, u32[]{:S(2)}) collective-permute-start(bf16[3,2,128,128]{3,2,1,0:T(8,128)(2,1)} %get-tuple-element.19), channel_id=1, source_target_pairs={{0,756},{12,0},{24,12},{36,24},{48,36},{60,48},{72,60},{84,72},{96... | collective-permute-start | bytes 589832 | tf_op jit(solution)/shard_map/ppermute | solution.py:299
  29.4 50.4 %copy-start = (f32[128,64]{0,1:T(8,128)S(1)}, f32[128,64]{0,1:T(8,128)}, u32[]{:S(2)}) copy-start(f32[128,64]{0,1:T(8,128)} %param.7) | copy-start | bytes 98308
  29.4 50.4 %copy-start.1 = (s32[128]{0:T(128)S(1)}, s32[128]{0:T(128)}, u32[]{:S(2)}) copy-start(s32[128]{0:T(128)} %param.5) | copy-start | bytes 1540
